TPU v7x, 32 devices: a whole 2x2x4 slice. The times are simulated.
32 devices in a mesh: fsdp: 2 (over x), ctx: 4 (over y, core), tp: 4 (over z).
Axes of the slice: x: 2, y: 2, z: 4, core: 2. Of those that a mesh axis runs over, the one named last changes fastest.
Arguments:
- inputs: bfloat16 [4, 16, 196, 768], P('fsdp', 'ctx', 'tp'), may hold values from -6 to 6
- cotangent: bfloat16 [4, 16, 196, 768], P('fsdp', 'ctx', 'tp'), may hold values from -6 to 6
- norm_gain: float32 [3, 768], replicated, may hold values from 0.5 to 1.5
- norm_bias: float32 [3, 768], replicated, may hold values from -1 to 1
- attn_weight: bfloat16 [2, 3, 768, 768], P(None, None, 'fsdp', 'tp'), may hold values from -0.21875 to 0.21875
- attn_bias: float32 [2, 2, 768], P(None, None, 'tp'), may hold values from -1 to 1
- out_weight: bfloat16 [2, 768, 768], P(None, 'tp', 'fsdp'), may hold values from -0.625 to 0.625
- out_bias: float32 [2, 768], replicated, may hold values from -1 to 1
- up_weight: bfloat16 [768, 3072], P('fsdp', 'tp'), may hold values from -0.21875 to 0.21875
- up_bias: float32 [3072], replicated, may hold values from -1 to 1
- down_weight: bfloat16 [3072, 768], P('tp', 'fsdp'), may hold values from -0.109375 to 0.109375
- down_bias: float32 [768], replicated, may hold values from -1 to 1
Outputs:
- outputs: bfloat16 [4, 16, 196, 768], P('fsdp', 'ctx', 'tp')
- input_grad: bfloat16 [4, 16, 196, 768], P('fsdp', 'ctx', 'tp')
- grad_norm_gain: float32 [3, 768], replicated
- grad_norm_bias: float32 [3, 768], replicated
- grad_attn_weight: float32 [2, 3, 768, 768], P(None, None, ('fsdp', 'ctx'), 'tp')
- grad_attn_bias: float32 [2, 2, 768], P(None, None, 'tp')
- grad_out_weight: float32 [2, 768, 768], P(None, 'tp', ('fsdp', 'ctx'))
- grad_out_bias: float32 [2, 768], replicated
- grad_up_weight: float32 [768, 3072], P(('fsdp', 'ctx'), 'tp')
- grad_up_bias: float32 [3072], replicated
- grad_down_weight: float32 [3072, 768], P('tp', ('fsdp', 'ctx'))
- grad_down_bias: float32 [768], replicated
All inputs are finite; a program needn't handle non-finite values.
Results may differ from a plain program's by a relative error of at most 0.025.
Values may be sent and summed in bfloat16 or wider, within the bound.
A program may use at most 128 MiB of HBM per device.

v0:
```python
import jax
import jax.numpy as jnp
from jax import lax
from jax.sharding import PartitionSpec as P

HEAD = 64


EPSILON = 1e-06


def layer_norm(rows, gain, shift):
    centre = rows - jnp.mean(rows, axis=-1, keepdims=True)
    spread = jnp.mean(centre * centre, axis=-1, keepdims=True)
    return centre * lax.rsqrt(spread + EPSILON) * gain + shift


def gelu_exact(values):
    return jax.nn.gelu(values, approximate=False)


def split_heads(values):
    return values.reshape(values.shape[:-1] + (values.shape[-1] // HEAD, HEAD))


def einsum_forms(temporal):
    if temporal:
        return ("qbhe,kbhe->bhqk", "bhqk,kbhe->qbhe", "bhqk,qbhe->kbhe")
    return ("bqhe,bkhe->bhqk", "bhqk,bkhe->bqhe", "bhqk,bqhe->bkhe")


def scores_of(queries, key_rows, temporal):
    score_form = einsum_forms(temporal)[0]
    return jnp.einsum(score_form, queries, key_rows, preferred_element_type=jnp.float32) * 0.125


def attend(triple, temporal):
    mix_form = einsum_forms(temporal)[1]
    queries, key_rows, value_rows = (
        split_heads(triple[0]),
        split_heads(triple[1]),
        split_heads(triple[2]),
    )
    scores = scores_of(queries, key_rows, temporal)
    highest = jnp.max(scores, axis=-1, keepdims=True)
    log_total = highest + jnp.log(jnp.sum(jnp.exp(scores - highest), axis=-1, keepdims=True))
    weights = jnp.exp(scores - log_total).astype(jnp.bfloat16)
    mixed = jnp.einsum(mix_form, weights, value_rows, preferred_element_type=jnp.float32)
    return (mixed.reshape(triple.shape[1:]).astype(jnp.bfloat16), log_total)


def attend_back(triple, log_total, grad_mixed, temporal):
    score_form, mix_form, back_form = einsum_forms(temporal)
    queries, key_rows, value_rows = (
        split_heads(triple[0]),
        split_heads(triple[1]),
        split_heads(triple[2]),
    )
    probs = jnp.exp(scores_of(queries, key_rows, temporal) - log_total)
    weights = probs.astype(jnp.bfloat16)
    grad_heads = split_heads(grad_mixed)
    grad_probs = jnp.einsum(score_form, grad_heads, value_rows, preferred_element_type=jnp.float32)
    inner = jnp.sum(probs * grad_probs, axis=-1, keepdims=True)
    grad_scores = (probs * (grad_probs - inner)).astype(jnp.bfloat16)
    grad_query = (
        jnp.einsum(mix_form, grad_scores, key_rows, preferred_element_type=jnp.float32) * 0.125
    )
    grad_key = (
        jnp.einsum(back_form, grad_scores, queries, preferred_element_type=jnp.float32) * 0.125
    )
    grad_value = jnp.einsum(back_form, weights, grad_heads, preferred_element_type=jnp.float32)
    stacked = jnp.stack([grad_query, grad_key, grad_value]).astype(jnp.bfloat16)
    return stacked.reshape(triple.shape)


def local(
    inputs,
    cotangent,
    norm_gain,
    norm_bias,
    attn_weight,
    attn_bias,
    out_weight,
    out_bias,
    up_weight,
    up_bias,
    down_weight,
    down_bias,
):
    width = attn_weight.shape[3]
    hidden_width = up_weight.shape[1]
    model_width = inputs.shape[3]
    tp_rank = lax.axis_index("tp")
    up_wide, down_wide = (up_weight, down_weight)
    up_bias_used = lax.dynamic_slice_in_dim(up_bias, tp_rank * hidden_width, hidden_width, 0)
    used_hidden = up_wide.shape[1]

    def fetch_weights():
        return (
            lax.all_gather(attn_weight, "fsdp", axis=2, tiled=True),
            lax.all_gather(out_weight, "fsdp", axis=2, tiled=True),
            lax.all_gather(up_wide, "fsdp", axis=0, tiled=True),
            lax.all_gather(down_wide, "fsdp", axis=1, tiled=True),
        )

    def spread_rows(values):
        return lax.all_gather(values, "tp", axis=1, tiled=True)

    def sum_rows(values):
        return lax.psum_scatter(
            values.astype(jnp.bfloat16), "tp", scatter_dimension=1, tiled=True
        ).astype(jnp.float32)

    def spread_grads(values):
        return lax.all_gather(values, "tp", axis=1, tiled=True)

    def sum_grads(values):
        return lax.psum_scatter(
            values.astype(jnp.bfloat16), "tp", scatter_dimension=1, tiled=True
        ).astype(jnp.float32)

    def attn_forward(stream, index, weights_all, temporal):
        attn_full, out_full = (weights_all[0], weights_all[1])
        normed = spread_rows(
            layer_norm(stream, norm_gain[index], norm_bias[index]).astype(jnp.bfloat16)
        )
        zero_row = jnp.zeros((width,), jnp.float32)
        bias_rows = jnp.stack([attn_bias[index, 0], zero_row, attn_bias[index, 1]])
        triple = jnp.einsum(
            "fpd,jdc->jfpc", normed, attn_full[index], preferred_element_type=jnp.float32
        )
        triple = (triple + bias_rows[:, None, None, :]).astype(jnp.bfloat16)
        if temporal:
            triple = lax.all_to_all(triple, "ctx", split_axis=2, concat_axis=1, tiled=True)
        mixed, log_total = attend(triple, temporal)
        if temporal:
            mixed = lax.all_to_all(mixed, "ctx", split_axis=0, concat_axis=1, tiled=True)
        partial_out = jnp.einsum(
            "fpc,cd->fpd", mixed, out_full[index], preferred_element_type=jnp.float32
        )
        stream_next = stream + (sum_rows(partial_out) + out_bias[index])
        return (stream_next, (normed, triple, log_total, mixed))

    def attn_backward(stream, index, weights_all, kept, grad_stream, temporal):
        attn_full, out_full = (weights_all[0], weights_all[1])
        normed, triple, log_total, mixed = kept
        grad_branch = grad_stream.astype(jnp.bfloat16)
        grad_bias_out = jnp.sum(grad_branch.astype(jnp.float32), axis=(0, 1))
        grad_full = spread_grads(grad_branch)
        grad_weight_out = jnp.einsum(
            "fpc,fpd->cd", mixed, grad_full, preferred_element_type=jnp.float32
        )
        grad_mixed = jnp.einsum(
            "fpd,cd->fpc", grad_full, out_full[index], preferred_element_type=jnp.float32
        ).astype(jnp.bfloat16)
        if temporal:
            grad_mixed = lax.all_to_all(grad_mixed, "ctx", split_axis=1, concat_axis=0, tiled=True)
        grad_triple = attend_back(triple, log_total, grad_mixed, temporal)
        if temporal:
            grad_triple = lax.all_to_all(
                grad_triple, "ctx", split_axis=1, concat_axis=2, tiled=True
            )
        grad_weight_attn = jnp.einsum(
            "fpd,jfpc->jdc", normed, grad_triple, preferred_element_type=jnp.float32
        )
        column_sums = jnp.sum(grad_triple.astype(jnp.float32), axis=(1, 2))
        grad_bias_attn = jnp.stack([column_sums[0], column_sums[2]])
        grad_normed = sum_grads(
            jnp.einsum(
                "jfpc,jdc->fpd", grad_triple, attn_full[index], preferred_element_type=jnp.float32
            )
        )
        unused, pull = jax.vjp(layer_norm, stream, norm_gain[index], norm_bias[index])
        grad_input, grad_gain, grad_shift = pull(grad_normed)
        return (
            grad_stream + grad_input,
            (
                grad_gain,
                grad_shift,
                grad_weight_attn,
                grad_bias_attn,
                grad_weight_out,
                grad_bias_out,
            ),
        )

    def mlp_forward(stream, weights_all):
        up_full, down_full = (weights_all[2], weights_all[3])
        normed = layer_norm(stream, norm_gain[2], norm_bias[2]).astype(jnp.bfloat16)
        normed = spread_rows(normed)
        hidden = (
            jnp.einsum("fpd,dc->fpc", normed, up_full, preferred_element_type=jnp.float32)
            + up_bias_used
        )
        active = gelu_exact(hidden).astype(jnp.bfloat16)
        partial_out = jnp.einsum(
            "fpc,cd->fpd", active, down_full, preferred_element_type=jnp.float32
        )
        partial_out = sum_rows(partial_out)
        return (stream + (partial_out + down_bias), (normed, hidden, active))

    def mlp_backward(stream, weights_all, kept, grad_stream):
        up_full, down_full = (weights_all[2], weights_all[3])
        normed, hidden, active = kept
        grad_branch = grad_stream.astype(jnp.bfloat16)
        grad_bias_down = jnp.sum(grad_branch.astype(jnp.float32), axis=(0, 1))
        grad_full = spread_grads(grad_branch)
        grad_weight_down = jnp.einsum(
            "fpc,fpd->cd", active, grad_full, preferred_element_type=jnp.float32
        )
        grad_active = jnp.einsum(
            "fpd,cd->fpc", grad_full, down_full, preferred_element_type=jnp.float32
        )
        unused, pull_gelu = jax.vjp(gelu_exact, hidden)
        grad_hidden = pull_gelu(grad_active)[0].astype(jnp.bfloat16)
        grad_bias_up = jnp.sum(grad_hidden.astype(jnp.float32), axis=(0, 1))
        grad_weight_up = jnp.einsum(
            "fpd,fpc->dc", normed, grad_hidden, preferred_element_type=jnp.float32
        )
        grad_normed = jnp.einsum(
            "fpc,dc->fpd", grad_hidden, up_full, preferred_element_type=jnp.float32
        )
        grad_normed = sum_grads(grad_normed)
        unused_ln, pull = jax.vjp(layer_norm, stream, norm_gain[2], norm_bias[2])
        grad_input, grad_gain, grad_shift = pull(grad_normed)
        return (
            grad_stream + grad_input,
            (grad_gain, grad_shift, grad_weight_up, grad_bias_up, grad_weight_down, grad_bias_down),
        )

    def step(totals, pair):
        clip, grad_clip = pair
        forward_weights = fetch_weights()
        backward_weights = fetch_weights()
        stream_first = clip.astype(jnp.float32)
        stream_second, kept_spatial = attn_forward(stream_first, 0, forward_weights, False)
        stream_third, kept_temporal = attn_forward(stream_second, 1, forward_weights, True)
        result, kept_mlp = mlp_forward(stream_third, forward_weights)
        grad_third, mlp_terms = mlp_backward(
            stream_third, backward_weights, kept_mlp, grad_clip.astype(jnp.float32)
        )
        grad_second, temporal_terms = attn_backward(
            stream_second, 1, backward_weights, kept_temporal, grad_third, True
        )
        grad_first, spatial_terms = attn_backward(
            stream_first, 0, backward_weights, kept_spatial, grad_second, False
        )
        increments = (
            jnp.stack([spatial_terms[0], temporal_terms[0], mlp_terms[0]]),
            jnp.stack([spatial_terms[1], temporal_terms[1], mlp_terms[1]]),
            jnp.stack([spatial_terms[2], temporal_terms[2]]),
            jnp.stack([spatial_terms[3], temporal_terms[3]]),
            jnp.stack([spatial_terms[4], temporal_terms[4]]),
            jnp.stack([spatial_terms[5], temporal_terms[5]]),
            mlp_terms[2],
            mlp_terms[3],
            mlp_terms[4],
            mlp_terms[5],
        )
        totals = jax.tree.map(jnp.add, totals, increments)
        return (totals, (result.astype(jnp.bfloat16), grad_first.astype(jnp.bfloat16)))

    start = (
        jnp.zeros((3, model_width), jnp.float32),
        jnp.zeros((3, model_width), jnp.float32),
        jnp.zeros((2, 3, model_width, width), jnp.float32),
        jnp.zeros((2, 2, width), jnp.float32),
        jnp.zeros((2, width, model_width), jnp.float32),
        jnp.zeros((2, model_width), jnp.float32),
        jnp.zeros((model_width, used_hidden), jnp.float32),
        jnp.zeros((used_hidden,), jnp.float32),
        jnp.zeros((used_hidden, model_width), jnp.float32),
        jnp.zeros((model_width,), jnp.float32),
    )
    totals, stacked = lax.scan(step, start, (inputs, cotangent))
    up_total, down_total = (totals[6], totals[8])
    up_bias_full = lax.dynamic_update_slice_in_dim(
        jnp.zeros((hidden_width * lax.axis_size("tp"),), jnp.float32),
        totals[7],
        tp_rank * hidden_width,
        0,
    )
    matrices = (
        lax.psum_scatter(totals[2], ("fsdp", "ctx"), scatter_dimension=2, tiled=True),
        lax.psum_scatter(totals[4], ("fsdp", "ctx"), scatter_dimension=2, tiled=True),
        lax.psum_scatter(up_total, ("fsdp", "ctx"), scatter_dimension=0, tiled=True),
        lax.psum_scatter(down_total, ("fsdp", "ctx"), scatter_dimension=1, tiled=True),
    )
    attn_bias_full = lax.dynamic_update_slice_in_dim(
        jnp.zeros((2, 2, model_width), jnp.float32), totals[3], tp_rank * width, 2
    )
    vectors = lax.psum(
        (totals[0], totals[1], attn_bias_full, totals[5], up_bias_full, totals[9]),
        ("fsdp", "ctx", "tp"),
    )
    attn_bias_part = lax.dynamic_slice_in_dim(vectors[2], tp_rank * width, width, 2)
    return (
        stacked[0],
        stacked[1],
        vectors[0],
        vectors[1],
        matrices[0],
        attn_bias_part,
        matrices[1],
        vectors[3],
        matrices[2],
        vectors[4],
        matrices[3],
        vectors[5],
    )


def solution(mesh):
    return jax.shard_map(
        local,
        mesh=mesh,
        in_specs=(
            P("fsdp", "ctx", "tp", None),
            P("fsdp", "ctx", "tp", None),
            P(),
            P(),
            P(None, None, "fsdp", "tp"),
            P(None, None, "tp"),
            P(None, "tp", "fsdp"),
            P(),
            P("fsdp", "tp"),
            P(),
            P("tp", "fsdp"),
            P(),
        ),
        out_specs=(
            P("fsdp", "ctx", "tp", None),
            P("fsdp", "ctx", "tp", None),
            P(),
            P(),
            P(None, None, ("fsdp", "ctx"), "tp"),
            P(None, None, "tp"),
            P(None, "tp", ("fsdp", "ctx")),
            P(),
            P(("fsdp", "ctx"), "tp"),
            P(),
            P("tp", ("fsdp", "ctx")),
            P(),
        ),
        check_vma=False,
    )
```

profile of v0, /device:TPU:0, one launch (start us, length us, event | category | flops | bytes accessed | tf_op | source)
XLA Modules:
  0.0 1764.5 jit_solution(5922801304353576764)
XLA Ops:
  9.5 1556.7 %while.33 = (s32[]{:T(128)}, f32[3,768]{1,0:T(4,128)}, f32[3,768]{1,0:T(4,128)}, f32[2,3,768,192]{2,3,1,0:T(8,128)}, f32[2,2,192]{2,1,0:T(2,128)}, /*index=5*/f3...) while((s32[]{:T(128)}, f32[3,768]{1,0:T(4,128)}, ...), condition=%wide.region_37.0_spmd.clone, body=%wide.region_0.37_spmd.clone.sunk | while | flops 11599428608 | bytes 431165984 | solution.py:275
  16.6 14.6 all_gather.55
  31.2 15.2 all-gather.18.cloned.1.call-done
  46.4 34.4 %all-gather.16.cloned.1.call-done = bf16[4,196,768]{2,0,1:T(4,128)(2,1)} async-done(((bf16[4,49,768]{2,0,1:T(4,128)(2,1)}), bf16[4,196,768]{2,0,1:T(4,128)(2,1)}) %all-gather.16.cloned.1.call-update) | async-done | bytes 1204240 | tf_op jit(solution)/shard_map/while/body/eval_jaxpr/all_gather | solution.py:107
  90.2 54.9 %all-reduce.24.cloned.1.call-done = bf16[4,196,768]{2,0,1:T(4,128)(2,1)} async-done(((bf16[4,196,768]{2,0,1:T(4,128)(2,1)}), bf16[4,196,768]{2,0,1:T(4,128)(2,1)}) %all-reduce.24.cloned.1.call-update) | async-done | bytes 1204240 | tf_op jit(solution)/shard_map/while
  150.0 30.2 %all-gather.20.cloned.1.call-done = bf16[4,196,768]{2,0,1:T(4,128)(2,1)} async-done(((bf16[4,49,768]{2,0,1:T(4,128)(2,1)}), bf16[4,196,768]{2,0,1:T(4,128)(2,1)}) %all-gather.20.cloned.1.call-update) | async-done | bytes 1204240 | tf_op jit(solution)/shard_map/while/body/eval_jaxpr/all_gather | solution.py:107
  187.4 19.9 %all_to_all.74 = bf16[3,4,196,192]{3,1,0,2:T(4,128)(2,1)S(1)} all-to-all(bf16[3,4,196,192]{3,1,0,2:T(4,128)(2,1)} %copy.354), channel_id=1, replica_groups=mesh['fsdp'=2,'ctx'=4,'tp'=4] {'ctx'}, dimensions={2} | all-to-all | bytes 1806336 | tf_op jit(solution)/shard_map/while/body/eval_jaxpr/all_to_all | solution.py:134
  227.8 11.7 all_to_all.75
  246.1 54.7 %all-reduce.26.cloned.1.call-done = bf16[4,196,768]{2,0,1:T(4,128)(2,1)} async-done(((bf16[4,196,768]{2,0,1:T(4,128)(2,1)}), bf16[4,196,768]{2,0,1:T(4,128)(2,1)}) %all-reduce.26.cloned.1.call-update) | async-done | bytes 1204240 | tf_op jit(solution)/shard_map/while
  307.1 17.4 all-gather.14.cloned.1.call-done
  324.5 32.9 %all-gather.22.cloned.1.call-done = bf16[4,196,768]{2,0,1:T(4,128)(2,1)} async-done(((bf16[4,49,768]{2,0,1:T(4,128)(2,1)}), bf16[4,196,768]{2,0,1:T(4,128)(2,1)}) %all-gather.22.cloned.1.call-update) | async-done | bytes 1204240 | tf_op jit(solution)/shard_map/while/body/eval_jaxpr/all_gather | solution.py:107
  362.1 6.8 multiply_convert_fusion.6
  368.9 12.0 all-gather.24.cloned.1.call-done
  380.9 32.3 %all-gather.26.cloned.1.call-done = bf16[1,4,196,768]{3,1,0,2:T(4,128)(2,1)} async-done(((bf16[1,4,49,768]{3,1,0,2:T(4,128)(2,1)}), bf16[1,4,196,768]{3,1,0,2:T(4,128)(2,1)}) %all-gather.26.cloned.1.call-update) | async-done | bytes 1204240 | tf_op jit(solution)/shard_map/while/body/eval_jaxpr/all_gather | solution.py:115
  413.2 5.7 convert_reduce_fusion.20
  421.6 56.2 %all-reduce.28.cloned.1.call-done = bf16[4,196,768]{2,0,1:T(4,128)(2,1)} async-done(((bf16[4,196,768]{2,0,1:T(4,128)(2,1)}), bf16[4,196,768]{2,0,1:T(4,128)(2,1)}) %all-reduce.28.cloned.1.call-update) | async-done | bytes 1204240 | tf_op jit(solution)/shard_map/while
  485.3 30.2 %all-gather.28.cloned.1.call-done = bf16[4,196,768]{2,0,1:T(4,128)(2,1)} async-done(((bf16[4,49,768]{2,0,1:T(4,128)(2,1)}), bf16[4,196,768]{2,0,1:T(4,128)(2,1)}) %all-gather.28.cloned.1.call-update) | async-done | bytes 1204240 | tf_op jit(solution)/shard_map/while/body/eval_jaxpr/all_gather | solution.py:115
  520.2 11.1 all_to_all.76
  555.5 20.4 %all_to_all.77 = bf16[3,16,49,192]{3,2,0,1:T(8,128)(2,1)S(1)} all-to-all(bf16[3,16,49,192]{3,2,0,1:T(8,128)(2,1)S(1)} %copy.369), channel_id=1, replica_groups=mesh['fsdp'=2,'ctx'=4,'tp'=4] {'ctx'}, dimensions={1} | all-to-all | bytes 1806336 | tf_op jit(solution)/shard_map/while/body/eval_jaxpr/all_to_all | solution.py:160
  586.6 49.8 %all-reduce.30.cloned.1.call-done = bf16[4,196,768]{2,0,1:T(4,128)(2,1)} async-done(((bf16[4,196,768]{2,0,1:T(4,128)(2,1)}), bf16[4,196,768]{2,0,1:T(4,128)(2,1)}) %all-reduce.30.cloned.1.call-update) | async-done | bytes 1204240 | tf_op jit(solution)/shard_map/while
  657.7 17.9 %all-gather.30.cloned.1.call-done = bf16[4,196,768]{2,0,1:T(4,128)(2,1)} async-done(((bf16[4,49,768]{2,0,1:T(4,128)(2,1)}), bf16[4,196,768]{2,0,1:T(4,128)(2,1)}) %all-gather.30.cloned.1.call-update) | async-done | bytes 1204240 | tf_op jit(solution)/shard_map/while/body/eval_jaxpr/all_gather | solution.py:115
  695.0 86.4 %all-reduce.32.cloned.1.call-done = (bf16[4,196,768]{2,0,1:T(4,128)(2,1)}, bf16[4,196,768]{2,0,1:T(4,128)(2,1)}) async-done(((bf16[4,196,768]{2,0,1:T(4,128)(2,1)}, bf16[4,196,768]{2,0,1:T(4,128)(2,1)}), (bf16[4,196,768]{2,0,1:T(4,128)(2,1)}, bf16[4,196,768]{2,0,1:T(4,128)(2,1)})) %all-reduce.32.cloned.1.call-update) | async-done | bytes 2408464 | tf_op jit(solution)/shard_map/while
  794.9 15.3 all_gather.55
  810.3 13.1 all-gather.18.cloned.1.call-done
  823.3 31.8 %all-gather.16.cloned.1.call-done = bf16[4,196,768]{2,0,1:T(4,128)(2,1)} async-done(((bf16[4,49,768]{2,0,1:T(4,128)(2,1)}), bf16[4,196,768]{2,0,1:T(4,128)(2,1)}) %all-gather.16.cloned.1.call-update) | async-done | bytes 1204240 | tf_op jit(solution)/shard_map/while/body/eval_jaxpr/all_gather | solution.py:107
  864.6 54.9 %all-reduce.24.cloned.1.call-done = bf16[4,196,768]{2,0,1:T(4,128)(2,1)} async-done(((bf16[4,196,768]{2,0,1:T(4,128)(2,1)}), bf16[4,196,768]{2,0,1:T(4,128)(2,1)}) %all-reduce.24.cloned.1.call-update) | async-done | bytes 1204240 | tf_op jit(solution)/shard_map/while
  924.4 30.2 %all-gather.20.cloned.1.call-done = bf16[4,196,768]{2,0,1:T(4,128)(2,1)} async-done(((bf16[4,49,768]{2,0,1:T(4,128)(2,1)}), bf16[4,196,768]{2,0,1:T(4,128)(2,1)}) %all-gather.20.cloned.1.call-update) | async-done | bytes 1204240 | tf_op jit(solution)/shard_map/while/body/eval_jaxpr/all_gather | solution.py:107
  961.7 19.8 %all_to_all.74 = bf16[3,4,196,192]{3,1,0,2:T(4,128)(2,1)S(1)} all-to-all(bf16[3,4,196,192]{3,1,0,2:T(4,128)(2,1)} %copy.354), channel_id=1, replica_groups=mesh['fsdp'=2,'ctx'=4,'tp'=4] {'ctx'}, dimensions={2} | all-to-all | bytes 1806336 | tf_op jit(solution)/shard_map/while/body/eval_jaxpr/all_to_all | solution.py:134
  1002.0 11.7 all_to_all.75
  1020.3 54.7 %all-reduce.26.cloned.1.call-done = bf16[4,196,768]{2,0,1:T(4,128)(2,1)} async-done(((bf16[4,196,768]{2,0,1:T(4,128)(2,1)}), bf16[4,196,768]{2,0,1:T(4,128)(2,1)}) %all-reduce.26.cloned.1.call-update) | async-done | bytes 1204240 | tf_op jit(solution)/shard_map/while
  1080.9 17.8 %all-gather.14.cloned.1.call-done = bf16[768,768]{1,0:T(8,128)(2,1)} async-done(((bf16[384,768]{1,0:T(8,128)(2,1)}), bf16[768,768]{1,0:T(8,128)(2,1)}) %all-gather.14.cloned.1.call-update) | async-done | bytes 1179664 | tf_op jit(solution)/shard_map/while/body/eval_jaxpr/all_gather | solution.py:102
  1098.7 32.9 %all-gather.22.cloned.1.call-done = bf16[4,196,768]{2,0,1:T(4,128)(2,1)} async-done(((bf16[4,49,768]{2,0,1:T(4,128)(2,1)}), bf16[4,196,768]{2,0,1:T(4,128)(2,1)}) %all-gather.22.cloned.1.call-update) | async-done | bytes 1204240 | tf_op jit(solution)/shard_map/while/body/eval_jaxpr/all_gather | solution.py:107
  1136.3 6.8 multiply_convert_fusion.6
  1143.0 12.0 all-gather.24.cloned.1.call-done
  1155.1 32.3 %all-gather.26.cloned.1.call-done = bf16[1,4,196,768]{3,1,0,2:T(4,128)(2,1)} async-done(((bf16[1,4,49,768]{3,1,0,2:T(4,128)(2,1)}), bf16[1,4,196,768]{3,1,0,2:T(4,128)(2,1)}) %all-gather.26.cloned.1.call-update) | async-done | bytes 1204240 | tf_op jit(solution)/shard_map/while/body/eval_jaxpr/all_gather | solution.py:115
  1187.4 5.7 convert_reduce_fusion.20
  1195.8 56.2 %all-reduce.28.cloned.1.call-done = bf16[4,196,768]{2,0,1:T(4,128)(2,1)} async-done(((bf16[4,196,768]{2,0,1:T(4,128)(2,1)}), bf16[4,196,768]{2,0,1:T(4,128)(2,1)}) %all-reduce.28.cloned.1.call-update) | async-done | bytes 1204240 | tf_op jit(solution)/shard_map/while
  1259.5 30.2 %all-gather.28.cloned.1.call-done = bf16[4,196,768]{2,0,1:T(4,128)(2,1)} async-done(((bf16[4,49,768]{2,0,1:T(4,128)(2,1)}), bf16[4,196,768]{2,0,1:T(4,128)(2,1)}) %all-gather.28.cloned.1.call-update) | async-done | bytes 1204240 | tf_op jit(solution)/shard_map/while/body/eval_jaxpr/all_gather | solution.py:115
  1294.4 11.3 all_to_all.76
  1329.9 20.4 %all_to_all.77 = bf16[3,16,49,192]{3,2,0,1:T(8,128)(2,1)S(1)} all-to-all(bf16[3,16,49,192]{3,2,0,1:T(8,128)(2,1)S(1)} %copy.369), channel_id=1, replica_groups=mesh['fsdp'=2,'ctx'=4,'tp'=4] {'ctx'}, dimensions={1} | all-to-all | bytes 1806336 | tf_op jit(solution)/shard_map/while/body/eval_jaxpr/all_to_all | solution.py:160
  1361.0 49.8 %all-reduce.30.cloned.1.call-done = bf16[4,196,768]{2,0,1:T(4,128)(2,1)} async-done(((bf16[4,196,768]{2,0,1:T(4,128)(2,1)}), bf16[4,196,768]{2,0,1:T(4,128)(2,1)}) %all-reduce.30.cloned.1.call-update) | async-done | bytes 1204240 | tf_op jit(solution)/shard_map/while
  1432.2 18.0 %all-gather.30.cloned.1.call-done = bf16[4,196,768]{2,0,1:T(4,128)(2,1)} async-done(((bf16[4,49,768]{2,0,1:T(4,128)(2,1)}), bf16[4,196,768]{2,0,1:T(4,128)(2,1)}) %all-gather.30.cloned.1.call-update) | async-done | bytes 1204240 | tf_op jit(solution)/shard_map/while/body/eval_jaxpr/all_gather | solution.py:115
  1471.5 84.3 %all-reduce.32.cloned.1.call-done = (bf16[4,196,768]{2,0,1:T(4,128)(2,1)}, bf16[4,196,768]{2,0,1:T(4,128)(2,1)}) async-done(((bf16[4,196,768]{2,0,1:T(4,128)(2,1)}, bf16[4,196,768]{2,0,1:T(4,128)(2,1)}), (bf16[4,196,768]{2,0,1:T(4,128)(2,1)}, bf16[4,196,768]{2,0,1:T(4,128)(2,1)})) %all-reduce.32.cloned.1.call-update) | async-done | bytes 2408464 | tf_op jit(solution)/shard_map/while
  1574.9 5.7 copy.195
  1581.7 40.8 %all-reduce.7 = (f32[3,768]{1,0:T(4,128)}, f32[3,768]{1,0:T(4,128)}, f32[2,2,768]{2,1,0:T(2,128)S(1)}, f32[2,768]{1,0:T(2,128)}, f32[3072]{0:T(1024)}, /*index=5*/f32[768]{0:T(1024)}) all-reduce(f32[3,768]{1,0:T(4,128)S(1)} %copy-done.64, f32[3,768]{1,0:T(4,128)S(1)} %copy-done.67, ...), channel_id=1, replica_groups=mesh['fsdp'=2,'ctx'=4,'tp'=4] {'fsdp','ctx','tp'}, use_global_device_ids=true, to_apply=%region_38.0 | all-reduce | flops 13056 | bytes 104448 | tf_op jit(solution)/shard_map/psum | solution.py:292
  1625.0 27.9 %reduce-scatter.11.cloned.1.call-done = f32[768,96]{0,1:T(8,128)} async-done(((f32[768,768]{0,1:T(8,128)}), f32[768,96]{0,1:T(8,128)}) %reduce-scatter.11.cloned.1.call-update) | async-done | bytes 294928 | tf_op jit(solution)/shard_map/reduce_scatter | solution.py:287
  1652.9 46.1 %reduce-scatter.9.cloned.1.call-done = f32[96,768]{1,0:T(8,128)} async-done(((f32[768,768]{1,0:T(8,128)}), f32[96,768]{1,0:T(8,128)}) %reduce-scatter.9.cloned.1.call-update) | async-done | bytes 294928 | tf_op jit(solution)/shard_map/reduce_scatter | solution.py:286
  1699.0 57.6 %reduce-scatter.7.cloned.1.call-done = f32[2,3,96,192]{3,2,1,0:T(8,128)} async-done(((f32[2,3,768,192]{3,2,1,0:T(8,128)}), f32[2,3,96,192]{3,2,1,0:T(8,128)}) %reduce-scatter.7.cloned.1.call-update) | async-done | bytes 442384 | tf_op jit(solution)/shard_map/reduce_scatter | solution.py:284
  (734 shorter events, 337.5 us)
Async XLA Ops:
  9.8 36.6 %all-gather.18.cloned.1.call-start = ((), (), s32[]{:S(2)}) async-start(), calls=%async_computation.14 | async-start | bytes 2654208 | tf_op jit(solution)/shard_map/while/body/eval_jaxpr/all_gather | solution.py:100
  10.5 70.2 %all-gather.16.cloned.1.call-start = ((), (), s32[]{:S(2)}) async-start(), calls=%async_computation.13 | async-start | bytes 1505280 | tf_op jit(solution)/shard_map/while/body/eval_jaxpr/all_gather | solution.py:107
  12.6 135.2 %copy-start.54 = (f32[768]{0:T(1024)}, f32[768]{0:T(1024)S(1)}, u32[]{:S(2)}) copy-start(f32[768]{0:T(1024)S(1)} %get-tuple-element.649) | copy-start | bytes 9220 | tf_op jit(solution)/shard_map/while
  16.5 128.7 %all-reduce.24.cloned.1.call-start = ((), (), s32[]{:S(2)}) async-start(), calls=%async_computation.15 | async-start | bytes 2408448 | tf_op jit(solution)/shard_map/while
  88.9 91.4 %all-gather.20.cloned.1.call-start = ((), (), s32[]{:S(2)}) async-start(), calls=%async_computation.16 | async-start | bytes 1505280 | tf_op jit(solution)/shard_map/while/body/eval_jaxpr/all_gather | solution.py:107
  149.9 150.9 %all-reduce.26.cloned.1.call-start = ((), (), s32[]{:S(2)}) async-start(), calls=%async_computation.17 | async-start | bytes 2408448 | tf_op jit(solution)/shard_map/while
  245.5 79.0 %all-gather.14.cloned.1.call-start = ((), (), s32[]{:S(2)}) async-start(), calls=%async_computation.12 | async-start | bytes 1769472 | tf_op jit(solution)/shard_map/while/body/eval_jaxpr/all_gather | solution.py:102
  246.1 111.3 %all-gather.22.cloned.1.call-start = ((), (), s32[]{:S(2)}) async-start(), calls=%async_computation.18 | async-start | bytes 1505280 | tf_op jit(solution)/shard_map/while/body/eval_jaxpr/all_gather | solution.py:107
  302.7 179.5 %copy-start.36 = (f32[4,49]{0,1:T(8,128)}, f32[4,49]{0,1:T(8,128)S(1)}, u32[]{:S(2)}) copy-start(f32[4,49]{0,1:T(8,128)S(1)} %fusion.242) | copy-start | bytes 2356 | tf_op jit(solution)/shard_map/while
  303.8 77.1 %all-gather.24.cloned.1.call-start = ((), (), s32[]{:S(2)}) async-start(), calls=%async_computation.19 | async-start | bytes 1769472 | tf_op jit(solution)/shard_map/while/body/eval_jaxpr/all_gather | solution.py:103
  304.5 108.6 %all-gather.26.cloned.1.call-start = ((), (), s32[]{:S(2)}) async-start(), calls=%async_computation.20 | async-start | bytes 1505280 | tf_op jit(solution)/shard_map/while/body/eval_jaxpr/all_gather | solution.py:115
  306.4 171.4 %all-reduce.28.cloned.1.call-start = ((), (), s32[]{:S(2)}) async-start(), calls=%async_computation.21 | async-start | bytes 2408448 | tf_op jit(solution)/shard_map/while
  421.5 94.0 %all-gather.28.cloned.1.call-start = ((), (), s32[]{:S(2)}) async-start(), calls=%async_computation.22 | async-start | bytes 1505280 | tf_op jit(solution)/shard_map/while/body/eval_jaxpr/all_gather | solution.py:115
  485.2 151.1 %all-reduce.30.cloned.1.call-start = ((), (), s32[]{:S(2)}) async-start(), calls=%async_computation.23 | async-start | bytes 2408448 | tf_op jit(solution)/shard_map/while
  581.0 94.7 %all-gather.30.cloned.1.call-start = ((), (), s32[]{:S(2)}) async-start(), calls=%async_computation.24 | async-start | bytes 1505280 | tf_op jit(solution)/shard_map/while/body/eval_jaxpr/all_gather | solution.py:115
  645.3 136.0 %all-reduce.32.cloned.1.call-start = ((), (), s32[]{:S(2)}) async-start(), calls=%async_computation.25 | async-start | bytes 4816896 | tf_op jit(solution)/shard_map/while
  692.6 88.7 %copy-start.4 = (bf16[2,4,49,768]{3,1,2,0:T(4,128)(2,1)S(1)}, bf16[2,4,49,768]{3,1,2,0:T(4,128)(2,1)}, u32[]{:S(2)}) copy-start(bf16[2,4,49,768]{3,1,2,0:T(4,128)(2,1)} %get-tuple-element.787) | copy-start | bytes 1806340 | tf_op jit(solution)/shard_map/while
  692.6 88.7 %copy-start.57 = (f32[768]{0:T(1024)S(1)}, f32[768]{0:T(1024)}, u32[]{:S(2)}) copy-start(f32[768]{0:T(1024)} %copy-done.56) | copy-start | bytes 9220 | tf_op jit(solution)/shard_map/while
  692.6 90.1 %copy-start.51 = (f32[4,49]{0,1:T(8,128)S(1)}, f32[4,49]{0,1:T(8,128)}, u32[]{:S(2)}) copy-start(f32[4,49]{0,1:T(8,128)} %copy-done.50) | copy-start | bytes 2356 | tf_op jit(solution)/shard_map/while
  692.6 90.1 %copy-start.40 = (f32[4,49]{0,1:T(8,128)S(1)}, f32[4,49]{0,1:T(8,128)}, u32[]{:S(2)}) copy-start(f32[4,49]{0,1:T(8,128)} %copy-done.39) | copy-start | bytes 2356 | tf_op jit(solution)/shard_map/while
  692.7 91.9 %copy-start.89 = (f32[768]{0:T(1024)S(1)}, f32[768]{0:T(1024)}, u32[]{:S(2)}) copy-start(f32[768]{0:T(1024)} %get-tuple-element.798) | copy-start | bytes 9220 | tf_op jit(solution)/shard_map/while
  695.0 89.6 %copy-start.21 = (f32[4,49,768]{2,0,1:T(4,128)S(1)}, f32[4,49,768]{2,0,1:T(4,128)}, u32[]{:S(2)}) copy-start(f32[4,49,768]{2,0,1:T(4,128)} %get-tuple-element.706) | copy-start | bytes 1806340 | tf_op jit(solution)/shard_map/while
  788.2 35.1 %all-gather.18.cloned.1.call-start = ((), (), s32[]{:S(2)}) async-start(), calls=%async_computation.14 | async-start | bytes 2654208 | tf_op jit(solution)/shard_map/while/body/eval_jaxpr/all_gather | solution.py:100
  788.8 66.3 %all-gather.16.cloned.1.call-start = ((), (), s32[]{:S(2)}) async-start(), calls=%async_computation.13 | async-start | bytes 1505280 | tf_op jit(solution)/shard_map/while/body/eval_jaxpr/all_gather | solution.py:107
  790.9 131.3 %copy-start.54 = (f32[768]{0:T(1024)}, f32[768]{0:T(1024)S(1)}, u32[]{:S(2)}) copy-start(f32[768]{0:T(1024)S(1)} %get-tuple-element.649) | copy-start | bytes 9220 | tf_op jit(solution)/shard_map/while
  794.8 124.8 %all-reduce.24.cloned.1.call-start = ((), (), s32[]{:S(2)}) async-start(), calls=%async_computation.15 | async-start | bytes 2408448 | tf_op jit(solution)/shard_map/while
  863.3 91.3 %all-gather.20.cloned.1.call-start = ((), (), s32[]{:S(2)}) async-start(), calls=%async_computation.16 | async-start | bytes 1505280 | tf_op jit(solution)/shard_map/while/body/eval_jaxpr/all_gather | solution.py:107
  924.3 150.7 %all-reduce.26.cloned.1.call-start = ((), (), s32[]{:S(2)}) async-start(), calls=%async_computation.17 | async-start | bytes 2408448 | tf_op jit(solution)/shard_map/while
  1019.7 79.0 %all-gather.14.cloned.1.call-start = ((), (), s32[]{:S(2)}) async-start(), calls=%async_computation.12 | async-start | bytes 1769472 | tf_op jit(solution)/shard_map/while/body/eval_jaxpr/all_gather | solution.py:102
  1020.3 111.3 %all-gather.22.cloned.1.call-start = ((), (), s32[]{:S(2)}) async-start(), calls=%async_computation.18 | async-start | bytes 1505280 | tf_op jit(solution)/shard_map/while/body/eval_jaxpr/all_gather | solution.py:107
  1076.9 179.5 %copy-start.36 = (f32[4,49]{0,1:T(8,128)}, f32[4,49]{0,1:T(8,128)S(1)}, u32[]{:S(2)}) copy-start(f32[4,49]{0,1:T(8,128)S(1)} %fusion.242) | copy-start | bytes 2356 | tf_op jit(solution)/shard_map/while
  1078.0 77.1 %all-gather.24.cloned.1.call-start = ((), (), s32[]{:S(2)}) async-start(), calls=%async_computation.19 | async-start | bytes 1769472 | tf_op jit(solution)/shard_map/while/body/eval_jaxpr/all_gather | solution.py:103
  1078.7 108.6 %all-gather.26.cloned.1.call-start = ((), (), s32[]{:S(2)}) async-start(), calls=%async_computation.20 | async-start | bytes 1505280 | tf_op jit(solution)/shard_map/while/body/eval_jaxpr/all_gather | solution.py:115
  1080.7 171.4 %all-reduce.28.cloned.1.call-start = ((), (), s32[]{:S(2)}) async-start(), calls=%async_computation.21 | async-start | bytes 2408448 | tf_op jit(solution)/shard_map/while
  1195.7 94.0 %all-gather.28.cloned.1.call-start = ((), (), s32[]{:S(2)}) async-start(), calls=%async_computation.22 | async-start | bytes 1505280 | tf_op jit(solution)/shard_map/while/body/eval_jaxpr/all_gather | solution.py:115
  1259.4 151.4 %all-reduce.30.cloned.1.call-start = ((), (), s32[]{:S(2)}) async-start(), calls=%async_computation.23 | async-start | bytes 2408448 | tf_op jit(solution)/shard_map/while
  1355.4 94.7 %all-gather.30.cloned.1.call-start = ((), (), s32[]{:S(2)}) async-start(), calls=%async_computation.24 | async-start | bytes 1505280 | tf_op jit(solution)/shard_map/while/body/eval_jaxpr/all_gather | solution.py:115
  1419.8 136.0 %all-reduce.32.cloned.1.call-start = ((), (), s32[]{:S(2)}) async-start(), calls=%async_computation.25 | async-start | bytes 4816896 | tf_op jit(solution)/shard_map/while
  1467.1 88.7 %copy-start.4 = (bf16[2,4,49,768]{3,1,2,0:T(4,128)(2,1)S(1)}, bf16[2,4,49,768]{3,1,2,0:T(4,128)(2,1)}, u32[]{:S(2)}) copy-start(bf16[2,4,49,768]{3,1,2,0:T(4,128)(2,1)} %get-tuple-element.787) | copy-start | bytes 1806340 | tf_op jit(solution)/shard_map/while
  1467.1 88.7 %copy-start.57 = (f32[768]{0:T(1024)S(1)}, f32[768]{0:T(1024)}, u32[]{:S(2)}) copy-start(f32[768]{0:T(1024)} %copy-done.56) | copy-start | bytes 9220 | tf_op jit(solution)/shard_map/while
  1467.1 90.1 %copy-start.51 = (f32[4,49]{0,1:T(8,128)S(1)}, f32[4,49]{0,1:T(8,128)}, u32[]{:S(2)}) copy-start(f32[4,49]{0,1:T(8,128)} %copy-done.50) | copy-start | bytes 2356 | tf_op jit(solution)/shard_map/while
  1467.1 90.2 %copy-start.40 = (f32[4,49]{0,1:T(8,128)S(1)}, f32[4,49]{0,1:T(8,128)}, u32[]{:S(2)}) copy-start(f32[4,49]{0,1:T(8,128)} %copy-done.39) | copy-start | bytes 2356 | tf_op jit(solution)/shard_map/while
  1467.1 92.0 %copy-start.89 = (f32[768]{0:T(1024)S(1)}, f32[768]{0:T(1024)}, u32[]{:S(2)}) copy-start(f32[768]{0:T(1024)} %get-tuple-element.798) | copy-start | bytes 9220 | tf_op jit(solution)/shard_map/while
  1471.5 87.6 %copy-start.21 = (f32[4,49,768]{2,0,1:T(4,128)S(1)}, f32[4,49,768]{2,0,1:T(4,128)}, u32[]{:S(2)}) copy-start(f32[4,49,768]{2,0,1:T(4,128)} %get-tuple-element.706) | copy-start | bytes 1806340 | tf_op jit(solution)/shard_map/while
  1566.2 56.9 %reduce-scatter.13.cloned.1.call-start = ((), (), s32[]{:S(2)}) async-start(), calls=%async_computation.11 | async-start | bytes 1327104
  1571.1 81.9 %reduce-scatter.11.cloned.1.call-start = ((), (), s32[]{:S(2)}) async-start(), calls=%async_computation.10 | async-start | bytes 2654208 | tf_op jit(solution)/shard_map/reduce_scatter | solution.py:287
  1574.3 124.7 %reduce-scatter.9.cloned.1.call-start = ((), (), s32[]{:S(2)}) async-start(), calls=%async_computation.9 | async-start | bytes 2654208 | tf_op jit(solution)/shard_map/reduce_scatter | solution.py:286
  1574.9 181.7 %reduce-scatter.7.cloned.1.call-start = ((), (), s32[]{:S(2)}) async-start(), calls=%async_computation.8 | async-start | bytes 5308416 | tf_op jit(solution)/shard_map/reduce_scatter | solution.py:284
  (180 other events, 2109.3 us)
Sparse Core Ops, SparseCore 0:
  12.2 34.2 all-gather.17
  48.6 32.1 all-gather.15
  89.0 56.1 all-reduce.23
  150.1 30.1 all-gather.19
  245.6 55.1 all-reduce.25
  302.2 22.2 all-gather.13
  326.6 30.6 all-gather.21
  358.9 21.9 all-gather.23
  382.5 30.6 all-gather.25
  421.7 56.1 all-reduce.27
  485.3 30.1 all-gather.27
  581.1 55.1 all-reduce.29
  645.5 30.1 all-gather.29
  685.4 95.8 all-reduce.31
  790.3 33.0 all-gather.17
  825.3 29.7 all-gather.15
  863.4 56.0 all-reduce.23
  924.4 30.1 all-gather.19
  1019.8 55.1 all-reduce.25
  1076.4 22.2 all-gather.13
  1100.8 30.6 all-gather.21
  1133.1 21.9 all-gather.23
  1156.7 30.6 all-gather.25
  1195.9 56.1 all-reduce.27
  1259.5 30.1 all-gather.27
  1355.5 55.2 all-reduce.29
  1419.9 30.1 all-gather.29
  1459.9 95.9 all-reduce.31
Sparse Core Ops, SparseCore 1:
  1571.1 35.7 reduce-scatter.12
  1610.7 42.2 reduce-scatter.10
  1656.7 42.2 reduce-scatter.8
  1703.0 53.5 reduce-scatter.6
where the time goes:
time: 1770 us; the launch traced here: 1760 us
  waiting for transfers between devices  1180 us (67%)
  blocking collectives  197 us (11%)
  local copies, waits for them, and re-layouts  154 us (9%)
  matrix products  108 us (6%)
  other arithmetic  98.1 us (6%)
    while x38, waiting for transfers between devices  606 us
    all_gather x6, waiting for transfers between devices, spread_rows(): return lax.all_gather(values, 'tp', axis=1, tiled=True)  192 us
    all_gather x6, waiting for transfers between devices, spread_grads(): return lax.all_gather(values, 'tp', axis=1, tiled=True)  161 us
    reduce_scatter x1, waiting for transfers between devices, local(): lax.psum_scatter(totals[2], ('fsdp', 'ctx'), scatter_dimension=2, tiled=T...  57.6 us
    reduce_scatter x1, waiting for transfers between devices, local(): lax.psum_scatter(up_total, ('fsdp', 'ctx'), scatter_dimension=0, tiled=True)  46.1 us
    psum x1, blocking collectives, local(): lax.psum((totals[0], totals[1], attn_bias_full, totals[5], up_bias_full,...  40.8 us
    all_to_all x2, blocking collectives, attn_backward(): lax.all_to_all(grad_triple, 'ctx', split_axis=1, concat_axis=2, tiled=True)  40.7 us
    all_to_all x2, blocking collectives, attn_forward(): lax.all_to_all(triple, 'ctx', split_axis=2, concat_axis=1, tiled=True)  39.7 us
  transfers between devices with their start and end apart: 32, of which 31 were waited for; matrix products, arithmetic and copies ran while one was open for 6% of the time, Pallas kernels for 0%

commit v1 on v0

v1 whole, which is shorter than its diff:
```python
import jax
import jax.numpy as jnp
from jax import lax
from jax.sharding import PartitionSpec as P

HEAD = 64
EPSILON = 1e-06
BF = jnp.bfloat16
F32 = jnp.float32


def layer_norm(rows, gain, shift):
    centre = rows - jnp.mean(rows, axis=-1, keepdims=True)
    spread = jnp.mean(centre * centre, axis=-1, keepdims=True)
    return centre * lax.rsqrt(spread + EPSILON) * gain + shift


def gelu_exact(values):
    return jax.nn.gelu(values, approximate=False)


def dot(form, a, b):
    return jnp.einsum(form, a, b, preferred_element_type=F32)


def attend(q, k, v):
    scores = dot("hgqe,hgke->hgqk", q, k) * 0.125
    highest = jnp.max(scores, axis=-1, keepdims=True)
    log_total = highest + jnp.log(jnp.sum(jnp.exp(scores - highest), axis=-1, keepdims=True))
    weights = jnp.exp(scores - log_total).astype(BF)
    return dot("hgqk,hgke->hgqe", weights, v).astype(BF), log_total


def attend_back(q, k, v, log_total, grad):
    probs = jnp.exp(dot("hgqe,hgke->hgqk", q, k) * 0.125 - log_total)
    grad_probs = dot("hgqe,hgke->hgqk", grad, v)
    inner = jnp.sum(probs * grad_probs, axis=-1, keepdims=True)
    grad_scores = (probs * (grad_probs - inner)).astype(BF)
    grad_q = dot("hgqk,hgke->hgqe", grad_scores, k) * 0.125
    grad_k = dot("hgqk,hgqe->hgke", grad_scores, q) * 0.125
    grad_v = dot("hgqk,hgqe->hgke", probs.astype(BF), grad)
    return jnp.stack([grad_q, grad_k, grad_v]).astype(BF)


def local(
    inputs,
    cotangent,
    norm_gain,
    norm_bias,
    attn_weight,
    attn_bias,
    out_weight,
    out_bias,
    up_weight,
    up_bias,
    down_weight,
    down_bias,
):
    ranks_f, ranks_c, ranks_t = (lax.axis_size("fsdp"), lax.axis_size("ctx"), lax.axis_size("tp"))
    everyone = ("fsdp", "ctx", "tp")
    ctx_rank = lax.axis_index("ctx")
    tp_rank = lax.axis_index("tp")
    clips, frames, places, model = inputs.shape
    width = attn_weight.shape[3]
    hidden = up_weight.shape[1]
    heads = model // HEAD
    shards = ranks_f * ranks_c

    def gather_rows(shard):
        rows = shard.shape[0] // ranks_c
        part = lax.dynamic_slice_in_dim(shard, ctx_rank * rows, rows, 0)
        return lax.all_gather(part, everyone, axis=0, tiled=False).reshape(
            (ranks_f, ranks_c, ranks_t, rows, shard.shape[1])
        )

    def full_in(shard):
        whole = gather_rows(shard)
        return whole.transpose(0, 1, 3, 2, 4).reshape(shard.shape[0] * ranks_f, -1)

    def full_out(shard):
        whole = gather_rows(shard)
        return whole.transpose(2, 1, 3, 0, 4).reshape(shard.shape[0] * ranks_t, -1)

    qkv_full = []
    out_full = []
    for layer in range(2):
        packed = attn_weight[layer].transpose(1, 0, 2).reshape(attn_weight.shape[2], 3 * width)
        whole = full_in(packed).reshape(model, ranks_t, 3, width)
        qkv_full.append(whole.transpose(2, 0, 1, 3).reshape(3, model, ranks_t * width))
        out_full.append(full_out(out_weight[layer]))
    up_full = full_in(up_weight)
    down_full = full_out(down_weight)
    attn_bias_full = lax.all_gather(attn_bias, "tp", axis=2, tiled=True)

    total_frames = frames * ranks_c
    pairs = clips * places
    share = -(-pairs // ranks_c)

    def home_to_spatial(values):
        return lax.all_to_all(values, "tp", split_axis=1, concat_axis=2, tiled=True)

    def spatial_to_home(values):
        return lax.all_to_all(values, "tp", split_axis=2, concat_axis=1, tiled=True)

    def home_to_temporal(values):
        rows = values.transpose(1, 0, 2, 3).reshape(frames, pairs, model)
        rows = jnp.pad(rows, ((0, 0), (0, share * ranks_c - pairs), (0, 0)))
        return lax.all_to_all(rows, "ctx", split_axis=1, concat_axis=0, tiled=True)

    def temporal_to_home(values):
        rows = lax.all_to_all(values, "ctx", split_axis=0, concat_axis=1, tiled=True)[:, :pairs]
        return rows.reshape(frames, clips, places, model).transpose(1, 0, 2, 3)

    def heads_apart(values, temporal):
        apart = values.reshape(values.shape[:2] + (heads, HEAD))
        return apart.transpose(2, 1, 0, 3) if temporal else apart.transpose(2, 0, 1, 3)

    def heads_joined(values, temporal):
        joined = values.transpose(2, 1, 0, 3) if temporal else values.transpose(1, 2, 0, 3)
        return joined.reshape(joined.shape[:2] + (model,))

    def attn_forward(stream, index, temporal):
        normed = layer_norm(stream, norm_gain[index], norm_bias[index]).astype(BF)
        biases = (attn_bias_full[index, 0], 0.0, attn_bias_full[index, 1])
        triple = [
            heads_apart((dot("abd,dc->abc", normed, qkv_full[index][j]) + biases[j]).astype(BF), temporal)
            for j in range(3)
        ]
        mixed, log_total = attend(*triple)
        mixed = heads_joined(mixed, temporal)
        stream_next = stream + (dot("abc,cd->abd", mixed, out_full[index]) + out_bias[index])
        return stream_next, (normed, triple, log_total, mixed)

    def attn_backward(stream, index, kept, grad_stream, temporal):
        normed, triple, log_total, mixed = kept
        grad_branch = grad_stream.astype(BF)
        grad_bias_out = jnp.sum(grad_branch.astype(F32), axis=(0, 1))
        grad_weight_out = dot("abc,abd->cd", mixed, grad_branch)
        grad_mixed = dot("abd,cd->abc", grad_branch, out_full[index]).astype(BF)
        grad_triple = attend_back(*triple, log_total, heads_apart(grad_mixed, temporal))
        grad_triple = [heads_joined(grad_triple[j], temporal) for j in range(3)]
        grad_weight_attn = [dot("abd,abc->dc", normed, g) for g in grad_triple]
        sums = [jnp.sum(g.astype(F32), axis=(0, 1)) for g in grad_triple]
        grad_normed = sum(
            dot("abc,dc->abd", grad_triple[j], qkv_full[index][j]) for j in range(3)
        )
        unused, pull = jax.vjp(layer_norm, stream, norm_gain[index], norm_bias[index])
        grad_input, grad_gain, grad_shift = pull(grad_normed)
        return grad_stream + grad_input, (
            grad_gain,
            grad_shift,
            grad_weight_attn,
            jnp.stack([sums[0], sums[2]]),
            grad_weight_out,
            grad_bias_out,
        )

    first = home_to_spatial(inputs)
    spatial_shape = first.shape
    first = first.reshape((-1,) + first.shape[2:]).astype(F32)
    second, kept_spatial = attn_forward(first, 0, False)
    second = home_to_temporal(
        spatial_to_home(second.astype(BF).reshape(spatial_shape))
    ).astype(F32)
    third, kept_temporal = attn_forward(second, 1, True)
    normed = layer_norm(third, norm_gain[2], norm_bias[2]).astype(BF)
    units = dot("abd,dc->abc", normed, up_full) + up_bias
    active = gelu_exact(units).astype(BF)
    result = third + (dot("abc,cd->abd", active, down_full) + down_bias)
    outputs = temporal_to_home(result.astype(BF))

    grad_out = home_to_temporal(cotangent)
    grad_bias_down = jnp.sum(grad_out.astype(F32), axis=(0, 1))
    grad_weight_down = dot("abc,abd->cd", active, grad_out)
    grad_active = dot("abd,cd->abc", grad_out, down_full)
    unused, pull_gelu = jax.vjp(gelu_exact, units)
    grad_units = pull_gelu(grad_active)[0].astype(BF)
    grad_bias_up = jnp.sum(grad_units.astype(F32), axis=(0, 1))
    grad_weight_up = dot("abd,abc->dc", normed, grad_units)
    grad_normed = dot("abc,dc->abd", grad_units, up_full)
    unused, pull = jax.vjp(layer_norm, third, norm_gain[2], norm_bias[2])
    grad_third, gain_mlp, shift_mlp = pull(grad_normed)
    grad_third = grad_third + grad_out.astype(F32)

    def scatter(blocks):
        return lax.psum_scatter(blocks.astype(BF), everyone, scatter_dimension=0, tiled=False).astype(F32)

    def blocks_in(grad):
        rows, columns = grad.shape
        parts = grad.reshape(shards, rows // shards, ranks_t, columns // ranks_t)
        return parts.transpose(0, 2, 1, 3).reshape(shards * ranks_t, rows // shards, columns // ranks_t)

    def blocks_out(grad):
        rows, columns = grad.shape
        parts = grad.reshape(ranks_t, rows // ranks_t, shards, columns // shards)
        return parts.transpose(2, 0, 1, 3).reshape(shards * ranks_t, rows // ranks_t, columns // shards)

    own_up = scatter(blocks_in(grad_weight_up.astype(BF)))
    own_down = scatter(blocks_out(grad_weight_down.astype(BF)))

    grad_second, temporal_terms = attn_backward(second, 1, kept_temporal, grad_third, True)
    grad_second = home_to_spatial(temporal_to_home(grad_second.astype(BF)))
    grad_second = grad_second.reshape(first.shape).astype(F32)
    grad_first, spatial_terms = attn_backward(first, 0, kept_spatial, grad_second, False)
    input_grad = spatial_to_home(grad_first.astype(BF).reshape(spatial_shape))

    own_attn = []
    own_out = []
    for terms in (spatial_terms, temporal_terms):
        own_attn.append(
            scatter(jnp.stack([blocks_in(g.astype(BF)) for g in terms[2]], axis=1))
        )
        own_out.append(scatter(blocks_out(terms[4].astype(BF))))

    vectors = lax.psum(
        (
            jnp.stack([spatial_terms[0], temporal_terms[0], gain_mlp]),
            jnp.stack([spatial_terms[1], temporal_terms[1], shift_mlp]),
            jnp.stack([spatial_terms[3], temporal_terms[3]]),
            jnp.stack([spatial_terms[5], temporal_terms[5]]),
            grad_bias_up,
            grad_bias_down,
        ),
        everyone,
    )
    attn_bias_part = lax.dynamic_slice_in_dim(vectors[2], tp_rank * width, width, 2)
    return (
        outputs,
        input_grad,
        vectors[0],
        vectors[1],
        jnp.stack(own_attn),
        attn_bias_part,
        jnp.stack(own_out),
        vectors[3],
        own_up,
        vectors[4],
        own_down,
        vectors[5],
    )


def solution(mesh):
    return jax.shard_map(
        local,
        mesh=mesh,
        in_specs=(
            P("fsdp", "ctx", "tp", None),
            P("fsdp", "ctx", "tp", None),
            P(),
            P(),
            P(None, None, "fsdp", "tp"),
            P(None, None, "tp"),
            P(None, "tp", "fsdp"),
            P(),
            P("fsdp", "tp"),
            P(),
            P("tp", "fsdp"),
            P(),
        ),
        out_specs=(
            P("fsdp", "ctx", "tp", None),
            P("fsdp", "ctx", "tp", None),
            P(),
            P(),
            P(None, None, ("fsdp", "ctx"), "tp"),
            P(None, None, "tp"),
            P(None, "tp", ("fsdp", "ctx")),
            P(),
            P(("fsdp", "ctx"), "tp"),
            P(),
            P("tp", ("fsdp", "ctx")),
            P(),
        ),
        check_vma=False,
    )
```

time: 1770 us -> 1170 us (0.66)
  waiting for transfers between devices: 1180 us -> 620 us
  blocking collectives: 197 us -> 73.4 us
  local copies, waits for them, and re-layouts: 154 us -> 259 us
  other arithmetic: 98.1 us -> 40.7 us
  starting transfers between devices: 2.54 us -> 34.3 us
    while x38 -> x0, waiting for transfers between devices: 606 us -> none
    all_gather x18 -> x6, waiting for transfers between devices: 441 us -> 159 us  [gather_rows(): lax.all_gather(part, everyone, axis=0, tiled=False)]
    reduce_scatter x3 -> x6, waiting for transfers between devices: 132 us -> 413 us  [scatter(): lax.psum_scatter(blocks.astype(BF), everyone, scatter_dimension=0, tiled=...]
    all_to_all x8 -> x0, blocking collectives: 126 us -> none  [the longest x2 40.7 us: attn_backward(): lax.all_to_all(grad_triple, 'ctx', split_axis=1, concat_axis=2, tiled=True)]
    reshape x2 -> x28, local copies, waits for them, and re-layouts: 4.73 us -> 117 us  [the longest x7 32.2 us: blocks_in(): parts = grad.reshape(shards, rows // shards, ranks_t, columns // ranks_t)]
    all_to_all x0 -> x8, waiting for transfers between devices: none -> 47.3 us  [the longest x2 17.7 us: spatial_to_home(): return lax.all_to_all(values, 'tp', split_axis=2, concat_axis=1, tiled=True)]
    transpose x2 -> x20, local copies, waits for them, and re-layouts: 4.72 us -> 51.1 us  [the longest x7 18.5 us: blocks_in(): parts.transpose(0, 2, 1, 3)]
    while x384 -> x0, local copies, waits for them, and re-layouts: 34.9 us -> none
  transfers between devices with their start and end apart: 32 -> 20, of which waited for: 31 -> 14; matrix products, arithmetic and copies ran while one was open for 6% -> 26% of each run, Pallas kernels for 0% -> 0%
where the time goes in v1:
time: 1170 us; the launch traced here: 1160 us
  waiting for transfers between devices  620 us (53%)
  local copies, waits for them, and re-layouts  259 us (22%)
  matrix products  112 us (10%)
  blocking collectives  73.4 us (6%)
  other arithmetic  40.7 us (3%)
  starting transfers between devices  34.3 us (3%)
  between operations  16 us (1%)
    reduce_scatter x6, waiting for transfers between devices, scatter(): lax.psum_scatter(blocks.astype(BF), everyone, scatter_dimension=0, tiled=...  413 us
    all_gather x6, waiting for transfers between devices, gather_rows(): lax.all_gather(part, everyone, axis=0, tiled=False)  159 us
    dot_general x42, matrix products, dot(): return jnp.einsum(form, a, b, preferred_element_type=F32)  112 us
    psum x1, blocking collectives, local(): lax.psum((jnp.stack([spatial_terms[0], temporal_terms[0], gain_mlp]), jnp...  41.5 us
    reshape x7, local copies, waits for them, and re-layouts, blocks_in(): parts = grad.reshape(shards, rows // shards, ranks_t, columns // ranks_t)  32.2 us
    all_gather x1, blocking collectives, local(): attn_bias_full = lax.all_gather(attn_bias, 'tp', axis=2, tiled=True)  31.9 us
  transfers between devices with their start and end apart: 20, of which 14 were waited for; matrix products, arithmetic and copies ran while one was open for 26% of the time, Pallas kernels for 0%

profile of v1, /device:TPU:0, one launch (start us, length us, event | category | flops | bytes accessed | tf_op | source)
XLA Modules:
  0.0 1155.5 jit_solution(14739865770206832864)
XLA Ops:
  14.7 6.5 all-to-all-start
  23.0 31.9 %all_gather.37 = f32[2,2,768]{1,0,2:T(2,128)S(1)} all-gather(f32[2,2,192]{1,0,2:T(2,128)S(1)} %copy.749), channel_id=1, replica_groups=mesh['fsdp'=2,'ctx'=4,'tp'=4] {'tp'}, dimensions={2}, use_global_device_ids=true | all-gather | bytes 15360 | tf_op jit(solution)/shard_map/all_gather | solution.py:93
  55.0 10.7 slice_reduce_fusion.1
  76.0 59.1 %all-gather.15.cloned.1.call-done = bf16[3072,576]{1,0:T(8,128)(2,1)} async-done(((bf16[96,576]{1,0:T(8,128)(2,1)}), bf16[3072,576]{1,0:T(8,128)(2,1)}) %all-gather.15.cloned.1.call-update) | async-done | bytes 3538960 | tf_op jit(solution)/shard_map/all_gather | solution.py:72
  135.1 8.7 copy.746
  143.8 9.2 reshape_reshape.6
  153.0 3.7 fusion.84
  180.2 17.7 %all-to-all-done.1 = bf16[2,1,196,768]{3,0,1,2:T(2,128)(2,1)S(1)} async-done(((bf16[2,1,196,768]{3,0,1,2:T(2,128)(2,1)}), bf16[2,1,196,768]{3,0,1,2:T(2,128)(2,1)S(1)}, u32[]{:S(2)}, u32[]{:S(2)}) %all-to-all-start.1) | async-done | bytes 602144 | tf_op jit(solution)/shard_map/all_to_all | solution.py:103
  202.7 9.3 all-to-all-done.4
  212.0 3.9 all-to-all-start.2
  221.0 38.1 %all-gather.17.cloned.1.call-done = bf16[3072,576]{1,0:T(8,128)(2,1)} async-done(((bf16[96,576]{1,0:T(8,128)(2,1)}), bf16[3072,576]{1,0:T(8,128)(2,1)}) %all-gather.17.cloned.1.call-update) | async-done | bytes 3538960 | tf_op jit(solution)/shard_map/all_gather | solution.py:72
  259.1 8.8 copy.774
  267.9 9.2 reshape_reshape.7
  310.0 14.9 %all-gather.21.cloned.1.call-done = bf16[6144,384]{1,0:T(8,128)(2,1)} async-done(((bf16[192,384]{1,0:T(8,128)(2,1)}), bf16[6144,384]{1,0:T(8,128)(2,1)}) %all-gather.21.cloned.1.call-update) | async-done | bytes 4718608 | tf_op jit(solution)/shard_map/all_gather | solution.py:72
  324.9 9.3 copy.1006
  334.2 11.6 %reshape.560 = bf16[3072,768,1]{1,0,2:T(8,128)(2,1)} reshape(bf16[4,4,192,2,384]{4,3,2,1,0:T(2,128)(2,1)} %bitcast.279) | data formatting | bytes 9437184 | tf_op jit(solution)/shard_map/reshape | solution.py:82
  345.8 44.4 %all-gather.19.cloned.1.call-done = bf16[3072,768]{1,0:T(8,128)(2,1)} async-done(((bf16[96,768]{1,0:T(8,128)(2,1)}), bf16[3072,768]{1,0:T(8,128)(2,1)}) %all-gather.19.cloned.1.call-update) | async-done | bytes 4718608 | tf_op jit(solution)/shard_map/all_gather | solution.py:72
  390.2 8.1 copy.1007
  398.3 9.3 reshape.559
  407.6 7.2 fusion.8
  414.8 15.5 %multiply_convert_fusion = (bf16[16,25,3072]{2,1,0:T(8,128)(2,1)}, f32[16,25,3072]{2,1,0:T(8,128)S(1)}) fusion(f32[16,25,3072]{2,1,0:T(8,128)S(1)} %get-tuple-element.169, f32[3072]{0:T(1024)S(1)} %copy-done.70, u16[25,3072]{1,0:T(8,128)(2,1)S(1)} %get-tuple-element.109, u16[25,3072]{1,0:T(8,128)(2,1)S(1)} %get-tuple-element.108), kind=kLoop, calls=%fused_computation.11 | loop fusion | flops 87244800 | bytes 12607488 | tf_op jit(solution)/shard_map/convert_element_type | solution.py:168
  430.3 8.9 convert_reduce_fusion
  439.2 6.9 multiply_reduce_fusion.4
  453.8 3.6 multiply_reduce_fusion.2
  486.3 4.3 all-to-all-start.5
  497.4 4.8 all-to-all-done.5
  515.0 10.0 all-to-all-done.6
  528.0 4.0 reshape.529
  538.5 4.4 reshape.526
  547.8 4.4 reshape.528
  567.8 4.6 reshape.525
  575.4 3.9 multiply_reduce_fusion
  591.4 4.4 reshape.524
  601.7 6.6 bitcast_convert_fusion.1
  608.3 9.8 reshape.533
  618.1 5.4 copy.854
  623.6 6.8 bitcast_convert_fusion
  630.4 6.6 copy.855
  637.0 9.7 reshape.535
  646.8 5.6 copy.856
  653.9 6.9 add_convert_fusion.2
  660.8 4.6 all-to-all-start.3
  672.7 5.5 all-to-all-done.3
  685.3 41.5 %all-reduce.2 = (f32[3,768]{1,0:T(4,128)}, f32[3,768]{1,0:T(4,128)}, f32[2,2,768]{2,1,0:T(2,128)S(1)}, f32[2,768]{1,0:T(2,128)}, f32[3072]{0:T(1024)}, /*index=5*/f32[768]{0:T(1024)}) all-reduce(f32[3,768]{1,0:T(4,128)S(1)} %pad_maximum_fusion.2, ...), channel_id=1, replica_groups=mesh['fsdp'=2,'ctx'=4,'tp'=4] {'fsdp','ctx','tp'}, use_global_device_ids=true, to_apply=%region_21.22 | all-reduce | flops 13056 | bytes 104448 | tf_op jit(solution)/shard_map/psum | solution.py:215
  730.1 81.2 %reduce-scatter.9.cloned.1.call-done = bf16[1,3,96,192]{3,2,1,0:T(8,128)(2,1)} async-done(((bf16[32,3,96,192]{3,2,1,0:T(8,128)(2,1)}), bf16[1,3,96,192]{3,2,1,0:T(8,128)(2,1)}) %reduce-scatter.9.cloned.1.call-update) | async-done | bytes 110608 | tf_op jit(solution)/shard_map/reduce_scatter | solution.py:186
  811.3 111.7 %reduce-scatter.7.cloned.1.call-done = bf16[1,3,96,192]{3,2,1,0:T(8,128)(2,1)} async-done(((bf16[32,3,96,192]{3,2,1,0:T(8,128)(2,1)}), bf16[1,3,96,192]{3,2,1,0:T(8,128)(2,1)}) %reduce-scatter.7.cloned.1.call-update) | async-done | bytes 110608 | tf_op jit(solution)/shard_map/reduce_scatter | solution.py:186
  924.9 110.0 %reduce-scatter.15.cloned.1.call-done = bf16[1,96,768]{2,1,0:T(8,128)(2,1)} async-done(((bf16[32,96,768]{2,1,0:T(8,128)(2,1)}), bf16[1,96,768]{2,1,0:T(8,128)(2,1)}) %reduce-scatter.15.cloned.1.call-update) | async-done | bytes 147472 | tf_op jit(solution)/shard_map/reduce_scatter | solution.py:186
  1036.5 110.1 %reduce-scatter.17.cloned.1.call-done = bf16[1,768,96]{1,2,0:T(8,128)(2,1)} async-done(((bf16[32,768,96]{1,2,0:T(8,128)(2,1)}), bf16[1,768,96]{1,2,0:T(8,128)(2,1)}) %reduce-scatter.17.cloned.1.call-update) | async-done | bytes 147472 | tf_op jit(solution)/shard_map/reduce_scatter | solution.py:186
  (373 shorter events, 216.3 us)
Async XLA Ops:
  7.2 5.9 copy-start
  7.2 64.5 %all-gather.11.cloned.1.call-start = ((), (), s32[]{:S(2)}) async-start(), calls=%async_computation.14 | async-start | bytes 1216512 | tf_op jit(solution)/shard_map/all_gather | solution.py:72
  9.0 126.1 %all-gather.15.cloned.1.call-start = ((), (), s32[]{:S(2)}) async-start(), calls=%async_computation.22 | async-start | bytes 4055040 | tf_op jit(solution)/shard_map/all_gather | solution.py:72
  9.0 4.8 copy-start.53
  11.3 205.6 %all-gather.13.cloned.1.call-start = ((), (), s32[]{:S(2)}) async-start(), calls=%async_computation.15 | async-start | bytes 1216512 | tf_op jit(solution)/shard_map/all_gather | solution.py:72
  12.0 247.1 %all-gather.17.cloned.1.call-start = ((), (), s32[]{:S(2)}) async-start(), calls=%async_computation.23 | async-start | bytes 4055040 | tf_op jit(solution)/shard_map/all_gather | solution.py:72
  13.0 311.9 %all-gather.21.cloned.1.call-start = ((), (), s32[]{:S(2)}) async-start(), calls=%async_computation.25 | async-start | bytes 4866048 | tf_op jit(solution)/shard_map/all_gather | solution.py:72
  13.8 9.0 copy-start.75
  14.7 40.2 %copy-start.74 = (f32[2,768]{1,0:T(2,128)S(1)}, f32[2,768]{1,0:T(2,128)}, u32[]{:S(2)}) copy-start(f32[2,768]{1,0:T(2,128)} %param.19) | copy-start | bytes 18436
  14.7 40.2 %copy-start.72 = (f32[3,768]{1,0:T(4,128)S(1)}, f32[3,768]{1,0:T(4,128)}, u32[]{:S(2)}) copy-start(f32[3,768]{1,0:T(4,128)} %param.15) | copy-start | bytes 27652
  14.7 40.2 %copy-start.73 = (f32[3,768]{1,0:T(4,128)S(1)}, f32[3,768]{1,0:T(4,128)}, u32[]{:S(2)}) copy-start(f32[3,768]{1,0:T(4,128)} %param.14) | copy-start | bytes 27652
  14.7 51.0 %all-to-all-start = ((bf16[2,4,49,768]{3,2,0,1:T(8,128)(2,1)}), bf16[2,4,49,768]{3,2,0,1:T(8,128)(2,1)S(1)}, u32[]{:S(2)}, u32[]{:S(2)}) async-start(bf16[2,4,49,768]{3,2,0,1:T(8,128)(2,1)} %copy.742), calls=%async_computation | async-start | bytes 1376256 | tf_op jit(solution)/shard_map/all_to_all | solution.py:100
  21.2 369.0 %all-gather.19.cloned.1.call-start = ((), (), s32[]{:S(2)}) async-start(), calls=%async_computation.24 | async-start | bytes 4866048 | tf_op jit(solution)/shard_map/all_gather | solution.py:72
  55.0 12.2 %copy-start.59 = (f32[768]{0:T(1024)}, f32[768]{0:T(1024)S(1)}, u32[]{:S(2)}) copy-start(f32[768]{0:T(1024)S(1)} %get-tuple-element.188) | copy-start | bytes 9220
  55.0 352.6 %copy-start.78 = (f32[768]{0:T(1024)}, f32[768]{0:T(1024)S(1)}, u32[]{:S(2)}) copy-start(f32[768]{0:T(1024)S(1)} %get-tuple-element.128) | copy-start | bytes 9220
  69.0 103.2 %copy-start.4 = (f32[2,4,49,768]{3,0,2,1:T(2,128)}, f32[2,4,49,768]{3,0,2,1:T(2,128)S(1)}, u32[]{:S(2)}) copy-start(f32[2,4,49,768]{3,0,2,1:T(2,128)S(1)} %copy.743) | copy-start | bytes 3612676
  153.0 4.7 copy-start.54
  158.7 11.2 copy-start.11
  174.3 4.8 copy-start.58
  175.6 22.3 %all-to-all-start.1 = ((bf16[2,1,196,768]{3,0,1,2:T(2,128)(2,1)}), bf16[2,1,196,768]{3,0,1,2:T(2,128)(2,1)S(1)}, u32[]{:S(2)}, u32[]{:S(2)}) async-start(bf16[2,1,196,768]{3,0,1,2:T(2,128)(2,1)} %copy.765), calls=%async_computation.1 | async-start | bytes 1204224 | tf_op jit(solution)/shard_map/all_to_all | solution.py:103
  197.9 14.1 %all-to-all-start.4 = ((bf16[4,100,768]{2,0,1:T(4,128)(2,1)}), bf16[4,100,768]{2,0,1:T(4,128)(2,1)S(1)}, u32[]{:S(2)}, u32[]{:S(2)}) async-start(bf16[4,100,768]{2,0,1:T(4,128)(2,1)} %pad.8), calls=%async_computation.4 | async-start | bytes 1228800 | tf_op jit(solution)/shard_map/all_to_all | solution.py:108
  212.0 7.4 copy-start.20
  212.0 68.7 %all-to-all-start.2 = ((bf16[4,100,768]{2,0,1:T(4,128)(2,1)}), bf16[4,100,768]{2,0,1:T(4,128)(2,1)S(1)}, u32[]{:S(2)}, u32[]{:S(2)}) async-start(bf16[4,100,768]{2,0,1:T(4,128)(2,1)} %pad.7), calls=%async_computation.2 | async-start | bytes 1228800 | tf_op jit(solution)/shard_map/all_to_all | solution.py:108
  280.7 4.6 copy-start.24
  308.5 137.5 %copy-start.61 = (f32[16,25]{1,0:T(8,128)}, f32[16,25]{1,0:T(8,128)S(1)}, u32[]{:S(2)}) copy-start(f32[16,25]{1,0:T(8,128)S(1)} %broadcast_multiply_fusion.1) | copy-start | bytes 4804
  310.0 136.1 %copy-start.66 = (f32[16,25]{1,0:T(8,128)}, f32[16,25]{1,0:T(8,128)S(1)}, u32[]{:S(2)}) copy-start(f32[16,25]{1,0:T(8,128)S(1)} %fusion.71) | copy-start | bytes 4804
  398.3 9.3 copy-start.70
  414.8 15.5 %copy-start.13 = (bf16[4,4,25,768]{3,2,1,0:T(8,128)(2,1)S(1)}, bf16[4,4,25,768]{3,2,1,0:T(8,128)(2,1)}, u32[]{:S(2)}) copy-start(bf16[4,4,25,768]{3,2,1,0:T(8,128)(2,1)} %copy.794) | copy-start | bytes 1843204
  430.3 8.9 copy-start.18
  474.8 5.0 copy-start.25
  486.3 16.0 %all-to-all-start.5 = ((bf16[16,25,768]{2,1,0:T(8,128)(2,1)}), bf16[16,25,768]{2,1,0:T(8,128)(2,1)}, u32[]{:S(2)}, u32[]{:S(2)}) async-start(bf16[16,25,768]{2,1,0:T(8,128)(2,1)} %add_convert_fusion.1), calls=%async_computation.5 | async-start | bytes 1572864 | tf_op jit(solution)/shard_map/all_to_all | solution.py:111
  490.6 238.0 %reduce-scatter.13.cloned.1.call-start = ((), (), s32[]{:S(2)}) async-start(), calls=%async_computation.19 | async-start | bytes 1622016 | tf_op jit(solution)/shard_map/reduce_scatter | solution.py:186
  505.4 19.6 %all-to-all-start.6 = ((bf16[2,4,49,768]{3,0,2,1:T(2,128)(2,1)}), bf16[2,4,49,768]{3,0,2,1:T(2,128)(2,1)S(1)}, u32[]{:S(2)}, u32[]{:S(2)}) async-start(bf16[2,4,49,768]{3,0,2,1:T(2,128)(2,1)} %copy.812), calls=%async_computation.6 | async-start | bytes 1204224 | tf_op jit(solution)/shard_map/all_to_all | solution.py:100
  508.9 219.7 %reduce-scatter.11.cloned.1.call-start = ((), (), s32[]{:S(2)}) async-start(), calls=%async_computation.18 | async-start | bytes 1622016 | tf_op jit(solution)/shard_map/reduce_scatter | solution.py:186
  534.9 276.3 %reduce-scatter.9.cloned.1.call-start = ((), (), s32[]{:S(2)}) async-start(), calls=%async_computation.17 | async-start | bytes 4866048 | tf_op jit(solution)/shard_map/reduce_scatter | solution.py:186
  556.9 366.1 %reduce-scatter.7.cloned.1.call-start = ((), (), s32[]{:S(2)}) async-start(), calls=%async_computation.16 | async-start | bytes 4866048 | tf_op jit(solution)/shard_map/reduce_scatter | solution.py:186
  565.9 9.5 copy-start.12
  572.3 6.9 slice-start
  600.3 434.6 %reduce-scatter.15.cloned.1.call-start = ((), (), s32[]{:S(2)}) async-start(), calls=%async_computation.20 | async-start | bytes 4866048 | tf_op jit(solution)/shard_map/reduce_scatter | solution.py:186
  623.5 523.1 %reduce-scatter.17.cloned.1.call-start = ((), (), s32[]{:S(2)}) async-start(), calls=%async_computation.21 | async-start | bytes 4866048 | tf_op jit(solution)/shard_map/reduce_scatter | solution.py:186
  660.8 4.6 copy-start.65
  660.8 4.8 copy-start.26
  660.8 17.5 %all-to-all-start.3 = ((bf16[16,25,768]{2,1,0:T(8,128)(2,1)}), bf16[16,25,768]{2,1,0:T(8,128)(2,1)}, u32[]{:S(2)}, u32[]{:S(2)}) async-start(bf16[16,25,768]{2,1,0:T(8,128)(2,1)} %add_convert_fusion.2), calls=%async_computation.3 | async-start | bytes 1572864 | tf_op jit(solution)/shard_map/all_to_all | solution.py:111
  671.4 10.3 copy-start.77
  671.4 10.3 copy-start.76
  671.4 10.3 copy-start.68
  678.2 49.3 %all-to-all-start.7 = ((bf16[2,1,196,768]{3,0,1,2:T(2,128)(2,1)}), bf16[2,1,196,768]{3,0,1,2:T(2,128)(2,1)S(1)}, u32[]{:S(2)}, u32[]{:S(2)}) async-start(bf16[2,1,196,768]{3,0,1,2:T(2,128)(2,1)} %copy.836), calls=%async_computation.7 | async-start | bytes 1204224 | tf_op jit(solution)/shard_map/all_to_all | solution.py:103
  727.5 420.7 %copy-start.1 = (bf16[768,384]{1,0:T(8,128)(2,1)S(1)}, bf16[768,384]{1,0:T(8,128)(2,1)}, u32[]{:S(2)}) copy-start(bf16[768,384]{1,0:T(8,128)(2,1)} %param.22) | copy-start | bytes 1769476
  (55 other events, 106.2 us)
Sparse Core Ops, SparseCore 0:
  11.5 60.1 all-gather.10
  75.2 59.8 all-gather.14
  138.0 53.7 all-gather.12
  195.1 63.9 all-gather.16
  262.5 62.4 all-gather.20
  328.2 61.8 all-gather.18
  497.6 97.5 reduce-scatter.12
  600.4 99.0 reduce-scatter.10
  705.0 106.2 reduce-scatter.8
  816.6 106.3 reduce-scatter.6
  928.5 106.3 reduce-scatter.14
  1040.2 106.3 reduce-scatter.16

commit v2 on v1

--- a/solution.py
+++ b/solution.py
@@ -1,12 +1,419 @@
 import jax
 import jax.numpy as jnp
 from jax import lax
+from jax.experimental import pallas as pl
+from jax.experimental.pallas import tpu as pltpu
 from jax.sharding import PartitionSpec as P
 
 HEAD = 64
 EPSILON = 1e-06
 BF = jnp.bfloat16
 F32 = jnp.float32
+MESH = pl.DeviceIdType.MESH
+PIECES = 4
+ALL = ("fsdp", "ctx", "tp")
+
+
+def places_of(x, y, k, z):
+    return {
+        "x": (1 - x, y * 2 + k, z),
+        "y": (x, (1 - y) * 2 + k, z),
+        "core": (x, y * 2 + 1 - k, z),
+        "up": (x, y * 2 + k, z + 1),
+        "down": (x, y * 2 + k, z - 1),
+        "z1": (x, y * 2 + k, (z // 2) * 2 + 1 - z % 2),
+        "z2": (x, y * 2 + k, (z + 2) % 4),
+    }
+
+
+def meet(places, sides, z, last):
+    barrier = pltpu.get_barrier_semaphore()
+    for side in sides:
+        pl.semaphore_signal(barrier, inc=1, device_id=places[side], device_id_type=MESH)
+
+    @pl.when(z < last)
+    def _():
+        pl.semaphore_signal(barrier, inc=1, device_id=places["up"], device_id_type=MESH)
+
+    @pl.when(z > 0)
+    def _():
+        pl.semaphore_signal(barrier, inc=1, device_id=places["down"], device_id_type=MESH)
+
+    inner = (z > 0).astype(jnp.int32) + (z < last).astype(jnp.int32)
+    pl.semaphore_wait(barrier, len(sides) + inner)
+
+
+def maybe(when, action):
+    if when is None:
+        action()
+    else:
+        pl.when(when)(action)
+
+
+def gather_kernel(shard, whole, send_sem, recv_sem, local_sem):
+    x, c, z = lax.axis_index("fsdp"), lax.axis_index("ctx"), lax.axis_index("tp")
+    y, k = c // 2, c % 2
+    rows = shard.shape[1] // 4
+    width = shard.shape[2]
+    last = 3
+    places = places_of(x, y, k, z)
+
+    def spot(ref, piece, f, cc, t):
+        row = pl.multiple_of((f * 4 + cc) * rows, 16)
+        return ref.at[piece, pl.ds(row, rows), pl.ds(pl.multiple_of(t * width, 128), width)]
+
+    meet(places, ("x", "y", "core"), z, last)
+    local = []
+    for piece in range(PIECES):
+        row = pl.multiple_of(x * rows * 4, 16)
+        copy = pltpu.make_async_copy(
+            shard.at[piece],
+            whole.at[piece, pl.ds(row, rows * 4), pl.ds(pl.multiple_of(z * width, 128), width)],
+            local_sem.at[piece],
+        )
+        copy.start()
+        local.append(copy)
+
+    sent = []
+
+    def send(side, unit, mine=False, pieces=range(PIECES), when=None):
+        f, cc, t = unit
+        copies = []
+        for piece in pieces:
+            target = spot(whole, piece, f, cc, t)
+            source = shard.at[piece, pl.ds(pl.multiple_of(cc * rows, 16), rows)] if mine else target
+            number = sum(len(c) for w, c in sent) + len(copies)
+            copies.append(
+                pltpu.make_async_remote_copy(
+                    src_ref=source,
+                    dst_ref=target,
+                    send_sem=send_sem.at[number],
+                    recv_sem=recv_sem.at[(f * 4 + cc) * 4 + t, piece],
+                    device_id=places[side],
+                    device_id_type=MESH,
+                )
+            )
+        sent.append((when, copies))
+
+        def start():
+            for copy in copies:
+                copy.start()
+
+        maybe(when, start)
+
+    def arrived(unit, when=None):
+        f, cc, t = unit
+
+        def wait():
+            for piece in range(PIECES):
+                ref = spot(whole, piece, f, cc, t)
+                pltpu.make_async_copy(ref, ref, recv_sem.at[(f * 4 + cc) * 4 + t, piece]).wait()
+
+        maybe(when, wait)
+
+    other_y = (1 - y) * 2 + k
+    first, second = (0, 1), (2, 3)
+    me = (x, c, z)
+    send("up", me, True, when=z < last)
+    send("down", me, True, when=z > 0)
+    send("x", me, True)
+    send("x", (x, other_y, z), True)
+
+    def at(sign, d):
+        t = z + sign * d
+        return t, ((t >= 0) if sign < 0 else (t <= last))
+
+    def from_line(sign, d):
+        t, have = at(sign, d)
+        unit = (x, c, t)
+        arrived(unit, have)
+        if d < last:
+            if sign < 0:
+                send("up", unit, when=have & (z < last))
+            else:
+                send("down", unit, when=have & (z > 0))
+        for side in ("x", "y", "core"):
+            send(side, unit, when=have)
+
+    def from_plane(sign, d):
+        t, have = at(sign, d)
+        arrived((1 - x, c, t), have)
+        send("y", (1 - x, c, t), pieces=second, when=have)
+        send("core", (1 - x, c, t), when=have)
+        arrived((x, other_y, t), have)
+        send("x", (x, other_y, t), pieces=first, when=have)
+        send("core", (x, other_y, t), when=have)
+
+    def from_diagonal(sign, d):
+        t, have = at(sign, d)
+        arrived((1 - x, other_y, t), have)
+        send("core", (1 - x, other_y, t), when=have)
+
+    def both(action, d):
+        action(-1, d)
+        action(1, d)
+
+    both(from_line, 1)
+    arrived((1 - x, c, z))
+    send("core", (1 - x, c, z))
+    both(from_line, 2)
+    arrived((1 - x, other_y, z))
+    send("core", (1 - x, other_y, z))
+    both(from_plane, 1)
+    both(from_line, 3)
+    both(from_plane, 2)
+    both(from_diagonal, 1)
+    both(from_plane, 3)
+    both(from_diagonal, 2)
+    both(from_diagonal, 3)
+    for sign, d in ((-1, 1), (1, 1), (-1, 2), (1, 2), (-1, 3), (1, 3)):
+        t, have = at(sign, d)
+        for f in (x, 1 - x):
+            for yy in (y, 1 - y):
+                arrived((f, yy * 2 + 1 - k, t), have)
+    for yy in (y, 1 - y):
+        arrived((1 - x, yy * 2 + 1 - k, z))
+    for when, copies in sent:
+
+        def wait():
+            for copy in copies:
+                copy.wait_send()
+
+        maybe(when, wait)
+    for copy in local:
+        copy.wait()
+
+
+def gather(shard):
+    ranks = (lax.axis_size("fsdp"), lax.axis_size("ctx"), lax.axis_size("tp"))
+    rows, width = shard.shape[1:]
+    if ranks != (2, 4, 4):
+        part = rows // ranks[1]
+        mine = lax.dynamic_slice_in_dim(shard, lax.axis_index("ctx") * part, part, 1)
+        tall = lax.all_gather(mine, ("fsdp", "ctx"), axis=1, tiled=True)
+        return lax.all_gather(tall, "tp", axis=2, tiled=True)
+    return pl.pallas_call(
+        gather_kernel,
+        out_shape=jax.ShapeDtypeStruct((PIECES, rows * 2, width * 4), BF),
+        in_specs=[pl.BlockSpec(memory_space=pltpu.VMEM)],
+        out_specs=pl.BlockSpec(memory_space=pl.ANY),
+        scratch_shapes=[
+            pltpu.SemaphoreType.DMA((260,)),
+            pltpu.SemaphoreType.DMA((32, PIECES)),
+            pltpu.SemaphoreType.DMA((PIECES,)),
+        ],
+        compiler_params=pltpu.CompilerParams(collective_id=0, has_side_effects=True),
+        name="gather_weights",
+    )(shard)
+
+
+STEPS = 16
+
+
+def scatter_kernel(
+    g_ref, v_ref, out_ref, vout_ref, own, r1, r2, r3x, r3y, rup, rdn, vr, va,
+    own_sem, s1, q1, s2, q2, s3a, s3b, q3x, q3y, sz, qup, qdn, vs, vq,
+):
+    x, c, z = lax.axis_index("fsdp"), lax.axis_index("ctx"), lax.axis_index("tp")
+    y, k = c // 2, c % 2
+    rows, width = out_ref.shape[1:]
+    last = 3
+    places = places_of(x, y, k, z)
+    meet(places, ("x", "y", "core", "z2"), z, last)
+
+    def tp_of(s):
+        return (3 * s) % 4
+
+    def spot(f, yy, kk, s):
+        row = pl.multiple_of((f * 4 + yy * 2 + kk) * rows, 16)
+        column = pl.multiple_of(tp_of(s) * width, 128)
+        return g_ref.at[s // 4, pl.ds(row, rows), pl.ds(column, width)]
+
+    def remote(src, dst, send, recv, side):
+        return pltpu.make_async_remote_copy(
+            src_ref=src, dst_ref=dst, send_sem=send, recv_sem=recv,
+            device_id=places[side], device_id_type=MESH,
+        )
+
+    def core_copy(s, f, yy):
+        return remote(
+            spot(f, yy, 1 - k, s), r1.at[s, f, yy], s1.at[s, f, yy], q1.at[s, f, yy], "core"
+        )
+
+    def own_copy(s, f, yy):
+        return pltpu.make_async_copy(spot(f, yy, k, s), own.at[s, f, yy], own_sem.at[s, f, yy])
+
+    def diag_copy(s, side):
+        return remote(r1.at[s, 1 - x, 1 - y], r2.at[s], s2.at[s], q2.at[s], side)
+
+    def x_copy(s):
+        return remote(r1.at[s, 1 - x, y], r3x.at[s], s3a.at[s], q3x.at[s], "x")
+
+    def y_copy(s):
+        return remote(r1.at[s, x, 1 - y], r3y.at[s], s3b.at[s], q3y.at[s], "y")
+
+    def up_copy(s):
+        return remote(r1.at[s, x, y], rup.at[s], sz.at[s], qup.at[s], "up")
+
+    def down_copy(s):
+        return remote(r1.at[s, x, y], rdn.at[s], sz.at[s], qdn.at[s], "down")
+
+    sides = ("core", "x", "y", "z1", "z2")
+
+    def v_copy(j):
+        return remote(va.at[j], vr.at[j], vs.at[j], vq.at[j], sides[j])
+
+    quads = [(f, yy) for f in range(2) for yy in range(2)]
+
+    def start(s, carry):
+        for f, yy in quads:
+            core_copy(s, f, yy).start()
+            own_copy(s, f, yy).start()
+        return carry
+
+    lax.fori_loop(0, STEPS, start, 0)
+    va[0] = v_ref[...]
+    v_copy(0).start()
+
+    def chip_sum(s):
+        for f, yy in quads:
+            core_copy(s, f, yy).wait_recv()
+            own_copy(s, f, yy).wait()
+            r1[s, f, yy] = r1[s, f, yy] + own[s, f, yy]
+
+        @pl.when(s % 2 == 0)
+        def _():
+            diag_copy(s, "x").start()
+            x_copy(s).start()
+
+        @pl.when(s % 2 == 1)
+        def _():
+            diag_copy(s, "y").start()
+            y_copy(s).start()
+
+    def turn(s):
+        diag_copy(s, "x").wait_recv()
+
+        @pl.when(s % 2 == 0)
+        def _():
+            r1[s, x, 1 - y] = r1[s, x, 1 - y] + r2[s]
+            y_copy(s).start()
+
+        @pl.when(s % 2 == 1)
+        def _():
+            r1[s, 1 - x, y] = r1[s, 1 - x, y] + r2[s]
+            x_copy(s).start()
+
+    def plane_sum(s):
+        x_copy(s).wait_recv()
+        y_copy(s).wait_recv()
+        total = r1[s, x, y].astype(F32) + r3x[s].astype(F32) + r3y[s].astype(F32)
+        r1[s, x, y] = total.astype(BF)
+
+    def line(s, hop):
+        t = tp_of(s)
+
+        @pl.when((z < t) & (z == hop))
+        def _():
+            if hop > 0:
+                up_copy(s).wait_recv()
+                r1[s, x, y] = r1[s, x, y] + rup[s]
+            up_copy(s).start()
+
+        @pl.when((z > t) & (last - z == hop))
+        def _():
+            if hop > 0:
+                down_copy(s).wait_recv()
+                r1[s, x, y] = r1[s, x, y] + rdn[s]
+            down_copy(s).start()
+
+        far = z + (last - 2 * z) * ((last - 2 * z) > 0).astype(jnp.int32)
+
+        @pl.when((z == t) & (far == hop))
+        def _():
+            out_ref[s // 4] = r1[s, x, y].astype(F32)
+
+            @pl.when(z > 0)
+            def _():
+                up_copy(s).wait_recv()
+                out_ref[s // 4] = out_ref[s // 4] + rup[s].astype(F32)
+
+            @pl.when(z < last)
+            def _():
+                down_copy(s).wait_recv()
+                out_ref[s // 4] = out_ref[s // 4] + rdn[s].astype(F32)
+
+    def guard(action, s, *rest):
+        @pl.when((s >= 0) & (s < STEPS))
+        def _():
+            action(s, *rest)
+
+    def step(s, carry):
+        guard(chip_sum, s)
+        guard(turn, s - 1)
+        guard(plane_sum, s - 3)
+        for hop in range(4):
+            guard(line, s - 3 - hop, hop)
+        for j in range(5):
+
+            @pl.when(s == 2 + j)
+            def _():
+                v_copy(j).wait()
+                if j < 4:
+                    va[j + 1] = va[j] + vr[j]
+                    v_copy(j + 1).start()
+                else:
+                    vout_ref[...] = va[j] + vr[j]
+
+        return carry
+
+    lax.fori_loop(0, STEPS + 6, step, 0)
+
+    def finish(s, carry):
+        for f, yy in quads:
+            core_copy(s, f, yy).wait_send()
+        diag_copy(s, "x").wait_send()
+        x_copy(s).wait_send()
+        y_copy(s).wait_send()
+
+        @pl.when(z != tp_of(s))
+        def _():
+            up_copy(s).wait_send()
+
+        return carry
+
+    lax.fori_loop(0, STEPS, finish, 0)
+
+
+def scatter(grads, vectors):
+    ranks = (lax.axis_size("fsdp"), lax.axis_size("ctx"), lax.axis_size("tp"))
+    rows = grads.shape[1] // (ranks[0] * ranks[1])
+    width = grads.shape[2] // ranks[2]
+    if ranks != (2, 4, 4):
+        tall = lax.psum_scatter(grads, ("fsdp", "ctx"), scatter_dimension=1, tiled=True)
+        own = lax.psum_scatter(tall, "tp", scatter_dimension=2, tiled=True)
+        return own.astype(F32), lax.psum(vectors, ALL)
+    sub = (rows, width)
+    dma = pltpu.SemaphoreType.DMA
+    return pl.pallas_call(
+        scatter_kernel,
+        out_shape=(
+            jax.ShapeDtypeStruct((PIECES,) + sub, F32),
+            jax.ShapeDtypeStruct(vectors.shape, F32),
+        ),
+        in_specs=[pl.BlockSpec(memory_space=pl.ANY), pl.BlockSpec(memory_space=pltpu.VMEM)],
+        out_specs=[pl.BlockSpec(memory_space=pltpu.VMEM)] * 2,
+        scratch_shapes=[pltpu.VMEM((STEPS, 2, 2) + sub, BF)] * 2
+        + [pltpu.VMEM((STEPS,) + sub, BF)] * 5
+        + [pltpu.VMEM((5,) + vectors.shape, F32)] * 2
+        + [dma((STEPS, 2, 2))] * 3
+        + [dma((STEPS,))] * 9
+        + [dma((5,))] * 2,
+        compiler_params=pltpu.CompilerParams(
+            collective_id=1, has_side_effects=True, vmem_limit_bytes=48 * 2**20
+        ),
+        name="scatter_grads",
+    )(grads, vectors)
 
 
 def layer_norm(rows, gain, shift):
@@ -56,43 +463,35 @@
     down_weight,
     down_bias,
 ):
-    ranks_f, ranks_c, ranks_t = (lax.axis_size("fsdp"), lax.axis_size("ctx"), lax.axis_size("tp"))
-    everyone = ("fsdp", "ctx", "tp")
-    ctx_rank = lax.axis_index("ctx")
+    ranks_c, ranks_t = lax.axis_size("ctx"), lax.axis_size("tp")
     tp_rank = lax.axis_index("tp")
     clips, frames, places, model = inputs.shape
     width = attn_weight.shape[3]
-    hidden = up_weight.shape[1]
     heads = model // HEAD
-    shards = ranks_f * ranks_c
-
-    def gather_rows(shard):
-        rows = shard.shape[0] // ranks_c
-        part = lax.dynamic_slice_in_dim(shard, ctx_rank * rows, rows, 0)
-        return lax.all_gather(part, everyone, axis=0, tiled=False).reshape(
-            (ranks_f, ranks_c, ranks_t, rows, shard.shape[1])
-        )
-
-    def full_in(shard):
-        whole = gather_rows(shard)
-        return whole.transpose(0, 1, 3, 2, 4).reshape(shard.shape[0] * ranks_f, -1)
-
-    def full_out(shard):
-        whole = gather_rows(shard)
-        return whole.transpose(2, 1, 3, 0, 4).reshape(shard.shape[0] * ranks_t, -1)
-
-    qkv_full = []
-    out_full = []
+
+    shard = jnp.concatenate(
+        [
+            jnp.concatenate(
+                [
+                    attn_weight.transpose(0, 2, 1, 3).reshape(2, attn_weight.shape[2], 3 * width),
+                    out_weight.transpose(0, 2, 1),
+                ],
+                axis=2,
+            ),
+            up_weight[None],
+            down_weight.T[None],
+        ]
+    )
+    whole = gather(shard)
+    qkv_full, out_full = [], []
     for layer in range(2):
-        packed = attn_weight[layer].transpose(1, 0, 2).reshape(attn_weight.shape[2], 3 * width)
-        whole = full_in(packed).reshape(model, ranks_t, 3, width)
-        qkv_full.append(whole.transpose(2, 0, 1, 3).reshape(3, model, ranks_t * width))
-        out_full.append(full_out(out_weight[layer]))
-    up_full = full_in(up_weight)
-    down_full = full_out(down_weight)
+        blocks = whole[layer].reshape(model, ranks_t, 4, width)
+        qkv_full.append([blocks[:, :, j].reshape(model, model) for j in range(3)])
+        out_full.append(blocks[:, :, 3].reshape(model, model))
+    up_full = whole[2]
+    down_full = whole[3]
     attn_bias_full = lax.all_gather(attn_bias, "tp", axis=2, tiled=True)
 
-    total_frames = frames * ranks_c
     pairs = clips * places
     share = -(-pairs // ranks_c)
 
@@ -128,15 +527,15 @@
         ]
         mixed, log_total = attend(*triple)
         mixed = heads_joined(mixed, temporal)
-        stream_next = stream + (dot("abc,cd->abd", mixed, out_full[index]) + out_bias[index])
+        stream_next = stream + (dot("abc,dc->abd", mixed, out_full[index]) + out_bias[index])
         return stream_next, (normed, triple, log_total, mixed)
 
     def attn_backward(stream, index, kept, grad_stream, temporal):
         normed, triple, log_total, mixed = kept
         grad_branch = grad_stream.astype(BF)
         grad_bias_out = jnp.sum(grad_branch.astype(F32), axis=(0, 1))
-        grad_weight_out = dot("abc,abd->cd", mixed, grad_branch)
-        grad_mixed = dot("abd,cd->abc", grad_branch, out_full[index]).astype(BF)
+        grad_weight_out = dot("abc,abd->dc", mixed, grad_branch)
+        grad_mixed = dot("abd,dc->abc", grad_branch, out_full[index]).astype(BF)
         grad_triple = attend_back(*triple, log_total, heads_apart(grad_mixed, temporal))
         grad_triple = [heads_joined(grad_triple[j], temporal) for j in range(3)]
         grad_weight_attn = [dot("abd,abc->dc", normed, g) for g in grad_triple]
@@ -166,13 +565,13 @@
     normed = layer_norm(third, norm_gain[2], norm_bias[2]).astype(BF)
     units = dot("abd,dc->abc", normed, up_full) + up_bias
     active = gelu_exact(units).astype(BF)
-    result = third + (dot("abc,cd->abd", active, down_full) + down_bias)
+    result = third + (dot("abc,dc->abd", active, down_full) + down_bias)
     outputs = temporal_to_home(result.astype(BF))
 
     grad_out = home_to_temporal(cotangent)
     grad_bias_down = jnp.sum(grad_out.astype(F32), axis=(0, 1))
-    grad_weight_down = dot("abc,abd->cd", active, grad_out)
-    grad_active = dot("abd,cd->abc", grad_out, down_full)
+    grad_weight_down = dot("abc,abd->dc", active, grad_out)
+    grad_active = dot("abd,dc->abc", grad_out, down_full)
     unused, pull_gelu = jax.vjp(gelu_exact, units)
     grad_units = pull_gelu(grad_active)[0].astype(BF)
     grad_bias_up = jnp.sum(grad_units.astype(F32), axis=(0, 1))
@@ -182,61 +581,54 @@
     grad_third, gain_mlp, shift_mlp = pull(grad_normed)
     grad_third = grad_third + grad_out.astype(F32)
 
-    def scatter(blocks):
-        return lax.psum_scatter(blocks.astype(BF), everyone, scatter_dimension=0, tiled=False).astype(F32)
-
-    def blocks_in(grad):
-        rows, columns = grad.shape
-        parts = grad.reshape(shards, rows // shards, ranks_t, columns // ranks_t)
-        return parts.transpose(0, 2, 1, 3).reshape(shards * ranks_t, rows // shards, columns // ranks_t)
-
-    def blocks_out(grad):
-        rows, columns = grad.shape
-        parts = grad.reshape(ranks_t, rows // ranks_t, shards, columns // shards)
-        return parts.transpose(2, 0, 1, 3).reshape(shards * ranks_t, rows // ranks_t, columns // shards)
-
-    own_up = scatter(blocks_in(grad_weight_up.astype(BF)))
-    own_down = scatter(blocks_out(grad_weight_down.astype(BF)))
-
     grad_second, temporal_terms = attn_backward(second, 1, kept_temporal, grad_third, True)
     grad_second = home_to_spatial(temporal_to_home(grad_second.astype(BF)))
     grad_second = grad_second.reshape(first.shape).astype(F32)
     grad_first, spatial_terms = attn_backward(first, 0, kept_spatial, grad_second, False)
     input_grad = spatial_to_home(grad_first.astype(BF).reshape(spatial_shape))
 
-    own_attn = []
-    own_out = []
-    for terms in (spatial_terms, temporal_terms):
-        own_attn.append(
-            scatter(jnp.stack([blocks_in(g.astype(BF)) for g in terms[2]], axis=1))
-        )
-        own_out.append(scatter(blocks_out(terms[4].astype(BF))))
-
-    vectors = lax.psum(
-        (
-            jnp.stack([spatial_terms[0], temporal_terms[0], gain_mlp]),
-            jnp.stack([spatial_terms[1], temporal_terms[1], shift_mlp]),
-            jnp.stack([spatial_terms[3], temporal_terms[3]]),
-            jnp.stack([spatial_terms[5], temporal_terms[5]]),
-            grad_bias_up,
-            grad_bias_down,
-        ),
-        everyone,
+    def joined(terms):
+        parts = [g.astype(BF).reshape(model, ranks_t, width) for g in terms[2] + [terms[4]]]
+        return jnp.stack(parts, axis=2).reshape(model, -1)
+
+    grads = jnp.stack(
+        [
+            grad_weight_up.astype(BF),
+            grad_weight_down.astype(BF),
+            joined(temporal_terms),
+            joined(spatial_terms),
+        ]
     )
-    attn_bias_part = lax.dynamic_slice_in_dim(vectors[2], tp_rank * width, width, 2)
+    parts = [
+        jnp.stack([spatial_terms[0], temporal_terms[0], gain_mlp]),
+        jnp.stack([spatial_terms[1], temporal_terms[1], shift_mlp]),
+        jnp.stack([spatial_terms[3], temporal_terms[3]]),
+        jnp.stack([spatial_terms[5], temporal_terms[5]]),
+        grad_bias_up,
+        grad_bias_down,
+    ]
+    lines = [p.reshape(-1, model) for p in parts]
+    used = sum(line.shape[0] for line in lines)
+    vectors = jnp.pad(jnp.concatenate(lines), ((0, -used % 8), (0, 0)))
+    own, vectors = scatter(grads, vectors)
+    sums, start = [], 0
+    for part, line in zip(parts, lines):
+        sums.append(vectors[start : start + line.shape[0]].reshape(part.shape))
+        start += line.shape[0]
+    attn = own[jnp.array([3, 2])].reshape(2, own.shape[1], 4, width)
     return (
         outputs,
         input_grad,
-        vectors[0],
-        vectors[1],
-        jnp.stack(own_attn),
-        attn_bias_part,
-        jnp.stack(own_out),
-        vectors[3],
-        own_up,
-        vectors[4],
-        own_down,
-        vectors[5],
+        sums[0],
+        sums[1],
+        attn[:, :, :3].transpose(0, 2, 1, 3),
+        lax.dynamic_slice_in_dim(sums[2], tp_rank * width, width, 2),
+        attn[:, :, 3].transpose(0, 2, 1),
+        sums[3],
+        own[0],
+        sums[4],
+        own[1].T,
+        sums[5],
     )
 
 

time: 1170 us -> 598 us (0.51)
  waiting for transfers between devices: 620 us -> 28.9 us
  Pallas kernels: 0 us -> 191 us
  local copies, waits for them, and re-layouts: 259 us -> 125 us
  blocking collectives: 73.4 us -> 31 us
  matrix products: 112 us -> 127 us
  other arithmetic: 40.7 us -> 54.8 us
  between operations: 16 us -> 2.11 us
    reduce_scatter x6 -> x0, waiting for transfers between devices: 413 us -> none  [scatter(): lax.psum_scatter(blocks.astype(BF), everyone, scatter_dimension=0, tiled=...]
    pallas_call x0 -> x2, Pallas kernels: none -> 191 us  [the longest x1 98.6 us: scatter(): pl.pallas_call(scatter_kernel, out_shape=(jax.ShapeDtypeStruct((PIECES,)...]
    all_gather x6 -> x0, waiting for transfers between devices: 159 us -> none  [gather_rows(): lax.all_gather(part, everyone, axis=0, tiled=False)]
    reshape x18 -> x7, local copies, waits for them, and re-layouts: 95.7 us -> 3.37 us  [the longest x1 1.54 us: local(): attn_weight.transpose(0, 2, 1, 3)]
    transpose x12 -> x1, local copies, waits for them, and re-layouts: 46 us -> 0.85 us  [local(): own[1]]
    psum x1 -> x0, blocking collectives: 41.5 us -> none  [local(): lax.psum((jnp.stack([spatial_terms[0], temporal_terms[0], gain_mlp]), jnp...]
    slice x4 -> x10, local copies, waits for them, and re-layouts: 9.66 us -> 32.6 us  [the longest x3 21.9 us: local(): blocks = whole[layer].reshape(model, ranks_t, 4, width)]
    another operation x7 -> x3, other arithmetic: 8.74 us -> 24.1 us  [the longest x1 16.7 us: local(): jnp.stack([grad_weight_up.astype(BF), grad_weight_down.astype(BF), joined...]
  transfers between devices with their start and end apart: 20 -> 8, of which waited for: 14 -> 5; matrix products, arithmetic and copies ran while one was open for 26% -> 20% of each run, Pallas kernels for 0% -> 32%
where the time goes in v2:
time: 598 us; the launch traced here: 593 us
  Pallas kernels  191 us (32%)
  matrix products  127 us (21%)
  local copies, waits for them, and re-layouts  125 us (21%)
  other arithmetic  54.8 us (9%)
  starting transfers between devices  33.2 us (6%)
  blocking collectives  31 us (5%)
  waiting for transfers between devices  28.9 us (5%)
    dot_general x42, matrix products, dot(): return jnp.einsum(form, a, b, preferred_element_type=F32)  127 us
    pallas_call x1, Pallas kernels, scatter(): pl.pallas_call(scatter_kernel, out_shape=(jax.ShapeDtypeStruct((PIECES,)...  98.6 us
    pallas_call x1, Pallas kernels, gather(): pl.pallas_call(gather_kernel, out_shape=jax.ShapeDtypeStruct((PIECES, row...  92.3 us
    all_gather x1, blocking collectives, local(): attn_bias_full = lax.all_gather(attn_bias, 'tp', axis=2, tiled=True)  31 us
    slice x3, local copies, waits for them, and re-layouts, local(): blocks = whole[layer].reshape(model, ranks_t, 4, width)  21.9 us
    another operation x1, other arithmetic, local(): jnp.stack([grad_weight_up.astype(BF), grad_weight_down.astype(BF), joined...  16.7 us
    all_to_all x2, waiting for transfers between devices, spatial_to_home(): return lax.all_to_all(values, 'tp', split_axis=2, concat_axis=1, tiled=True)  15.9 us
    unnamed x140, local copies, waits for them, and re-layouts  15.9 us
  transfers between devices with their start and end apart: 8, of which 5 were waited for; matrix products, arithmetic and copies ran while one was open for 20% of the time, Pallas kernels for 32%

profile of v2, /device:TPU:0, one launch (start us, length us, event | category | flops | bytes accessed | tf_op | source)
XLA Modules:
  0.0 592.9 jit_solution(3508774253736223326)
XLA Ops:
  2.7 6.5 %all-to-all-start = ((bf16[2,4,49,768]{3,2,0,1:T(8,128)(2,1)}), bf16[2,4,49,768]{3,2,0,1:T(8,128)(2,1)S(1)}, u32[]{:S(2)}, u32[]{:S(2)}) async-start(bf16[2,4,49,768]{3,2,0,1:T(8,128)(2,1)} %copy.755), calls=%async_computation | async-start | bytes 1376256 | tf_op jit(solution)/shard_map/all_to_all | solution.py:499
  9.6 31.0 %all_gather.3 = f32[2,2,768]{1,0,2:T(2,128)S(1)} all-gather(f32[2,2,192]{1,0,2:T(2,128)S(1)} %copy.764), channel_id=1, replica_groups=mesh['fsdp'=2,'ctx'=4,'tp'=4] {'tp'}, dimensions={2}, use_global_device_ids=true | all-gather | bytes 15360 | tf_op jit(solution)/shard_map/all_gather | solution.py:493
  45.1 92.3 %gather_weights.1 = bf16[4,768,3072]{2,1,0:T(8,128)(2,1)} custom-call(bf16[4,384,768]{2,1,0:T(8,128)(2,1)} %pad_maximum_fusion.3.shard), custom_call_target="tpu_custom_call" | custom-call | tf_op jit(solution)/shard_map/gather_weights/pallas_call | solution.py:195
  137.4 8.2 %fusion.98 = (bf16[1,768,3072]{2,1,0:T(8,128)(2,1)}, bf16[1,768,3072]{2,1,0:T(8,128)(2,1)}) fusion(bf16[4,768,3072]{2,1,0:T(8,128)(2,1)} %gather_weights.1), kind=kLoop, calls=%fused_computation.214 | loop fusion | bytes 18874368 | tf_op jit(solution)/shard_map/slice | solution.py:488
  145.6 7.0 %copy.761 = bf16[1,768,3072]{1,2,0:T(8,128)(2,1)} copy(bf16[1,768,3072]{2,1,0:T(8,128)(2,1)} %get-tuple-element.144) | data formatting | bytes 9437184 | tf_op jit(solution)/shard_map/slice | solution.py:488
  152.7 10.7 %slice_reduce_fusion.1 = (f32[768]{0:T(1024)S(1)}, f32[768]{0:T(1024)S(1)}, f32[768]{0:T(1024)S(1)}, f32[768]{0:T(1024)S(1)}) fusion(f32[2,2,768]{1,0,2:T(2,128)S(1)} %all_gather.3), kind=kLoop, calls=%fused_computation.163 | loop fusion | bytes 24576 | tf_op jit(solution)/shard_map/slice | solution.py:523
  163.5 4.2 fusion.100
  176.6 15.9 %convolution_convert_fusion.7 = bf16[2,196,768]{2,1,0:T(8,128)(2,1)} fusion(bf16[768,768,1]{0,1,2:T(8,128)(2,1)} %bitcast.329, bf16[2,196,768]{2,0,1:T(2,128)(2,1)} %bitcast.377), kind=kOutput, calls=%fused_computation.112 | convolution fusion | flops 462723072 | bytes 2383872 | tf_op jit(solution)/shard_map/abd,dc->abc/dot_general | solution.py:430
  201.6 4.3 all-to-all-start.1
  206.9 15.9 %all-to-all-done.1 = bf16[2,1,196,768]{3,0,1,2:T(2,128)(2,1)S(1)} async-done(((bf16[2,1,196,768]{3,0,1,2:T(2,128)(2,1)}), bf16[2,1,196,768]{3,0,1,2:T(2,128)(2,1)S(1)}, u32[]{:S(2)}, u32[]{:S(2)}) %all-to-all-start.1) | async-done | bytes 602144 | tf_op jit(solution)/shard_map/all_to_all | solution.py:502
  222.8 3.5 all-to-all-start.4
  226.3 6.7 %copy.788 = bf16[1,768,3072]{1,2,0:T(8,128)(2,1)} copy(bf16[1,768,3072]{2,1,0:T(8,128)(2,1)} %get-tuple-element.143) | data formatting | bytes 9437184 | tf_op jit(solution)/shard_map/slice | solution.py:488
  236.0 3.5 all-to-all-start.2
  239.5 4.6 fusion.99
  246.1 3.1 all-to-all-done.2
  263.2 3.3 multiply_reduce_fusion.3
  270.4 3.9 reshape.483
  277.6 6.9 %fusion.22 = (u16[25,3072]{1,0:T(8,128)(2,1)S(1)}, u16[25,3072]{1,0:T(8,128)(2,1)S(1)}, f32[16,25,3072]{2,1,0:T(8,128)S(1)}) fusion(f32[3072]{0:T(1024)S(1)} %copy-done.50, bf16[4,768,3072]{2,1,0:T(8,128)(2,1)} %gather_weights.1, f32[16,25,768]{2,1,0:T(8,128)S(1)} %get-tuple-element.172, f32[768]{0:T(1024)S(1)} %get-tuple-element.132, ...), kind=kOutput, calls=%fused_computation.49 | convolution fusion | flops 1906022400 | bytes 11191424 | tf_op jit(solution)/shard_map/abd,dc->abc/dot_general | solution.py:430
  284.6 15.4 %multiply_convert_fusion = (bf16[16,25,3072]{2,1,0:T(8,128)(2,1)}, f32[16,25,3072]{2,1,0:T(8,128)}) fusion(f32[16,25,3072]{2,1,0:T(8,128)S(1)} %get-tuple-element.173, f32[3072]{0:T(1024)S(1)} %copy-done.50, u16[25,3072]{1,0:T(8,128)(2,1)S(1)} %get-tuple-element.113, u16[25,3072]{1,0:T(8,128)(2,1)S(1)} %get-tuple-element.112), kind=kLoop, calls=%fused_computation.13 | loop fusion | flops 87244800 | bytes 12607488 | tf_op jit(solution)/shard_map/convert_element_type | solution.py:567
  300.1 9.0 %convert_reduce_fusion = (f32[3072]{0:T(1024)S(1)}, bf16[16,25,3072]{2,1,0:T(8,128)(2,1)}) fusion(f32[16,25,3072]{2,1,0:T(8,128)} %get-tuple-element.142, bf16[16,25,768]{2,1,0:T(8,128)(2,1)S(1)} %bitcast.314, bf16[4,768,3072]{2,1,0:T(8,128)(2,1)S(1)} %bitcast.288, f32[16,25,3072]{2,1,0:T(8,128)} %copy-done.11, f32[3072]{0:T(1024)S(1)} %copy-done.50), kind=kOutput, calls=%fused_computation.11 | convolution fusion | flops 1908323328 | bytes 17817600 | tf_op jit(solution)/shard_map/abd,dc->abc/dot_general | solution.py:430
  309.1 5.1 multiply_reduce_fusion.4
  314.2 5.2 fusion.14
  324.2 3.1 reshape.425
  327.3 3.6 multiply_reduce_fusion.2
  339.9 3.5 fusion.54
  343.4 6.7 %fusion.15 = bf16[1,768,3072]{2,1,0:T(8,128)(2,1)} fusion(bf16[16,25,768]{2,1,0:T(8,128)(2,1)S(1)} %bitcast.315, bf16[16,25,3072]{2,1,0:T(8,128)(2,1)} %get-tuple-element.141), kind=kOutput, calls=%fused_computation.41 | convolution fusion | flops 1889796096 | bytes 7790592 | tf_op jit(solution)/shard_map/abc,abd->dc/dot_general | solution.py:430
  351.7 3.4 reshape.426
  355.1 3.2 fusion.56
  359.9 3.4 reshape.428
  363.4 3.5 fusion.93
  370.0 3.5 all-to-all-start.5
  373.5 7.3 %add_convert_fusion.2 = bf16[16,25,768]{2,1,0:T(8,128)(2,1)} fusion(f32[16,25,768]{2,1,0:T(8,128)} %copy-done.12, bf16[16,25,3072]{2,1,0:T(8,128)(2,1)} %get-tuple-element.141, bf16[4,768,3072]{2,1,0:T(8,128)(2,1)} %gather_weights.1, f32[768]{0:T(1024)S(1)} %copy-done.57), kind=kOutput, calls=%fused_computation.84 | convolution fusion | flops 1888358400 | bytes 10054656 | tf_op jit(solution)/shard_map/abc,dc->abd/dot_general | solution.py:430
  380.7 4.3 all-to-all-done.5
  385.0 3.5 all-to-all-start.3
  388.6 3.2 bitcast_convert_fusion.8
  395.7 4.4 all-to-all-done.3
  400.1 3.5 all-to-all-start.6
  409.2 3.5 pad_maximum_fusion.1
  412.6 6.7 %copy.868 = bf16[1,768,3072]{2,1,0:T(8,128)(2,1)} copy(bf16[1,768,3072]{1,2,0:T(8,128)(2,1)} %bitcast.298) | data formatting | bytes 9437184 | tf_op jit(solution)/shard_map/stack;reshape | solution.py:594
  425.2 4.5 convert_reduce_fusion.4
  429.7 3.8 multiply_reduce_fusion
  441.9 3.0 bitcast_convert_fusion.3
  445.1 3.0 bitcast_convert_fusion.4
  453.3 5.0 all-to-all-start.7
  458.4 3.8 pad_maximum_fusion.2
  462.2 6.7 %copy.869 = bf16[1,768,3072]{2,1,0:T(8,128)(2,1)} copy(bf16[1,768,3072]{1,2,0:T(8,128)(2,1)} %bitcast.299) | data formatting | bytes 9437184 | tf_op jit(solution)/shard_map/stack;reshape | solution.py:594
  469.1 16.7 %pad_maximum_fusion.g_ref = bf16[4,768,3072]{2,1,0:T(8,128)(2,1)} fusion(bf16[1,768,3072]{2,1,0:T(8,128)(2,1)} %copy.869, bf16[1,768,3072]{2,1,0:T(8,128)(2,1)} %copy.868, bf16[1,768,3072]{2,1,0:T(8,128)(2,1)} %fusion.15, bf16[1,768,3072]{2,1,0:T(8,128)(2,1)} %fusion.14), kind=kLoop, calls=%fused_computation.1 | loop fusion | flops 28311552 | bytes 37748736 | tf_op jit(solution)/shard_map/stack | solution.py:594
  485.9 98.6 %scatter_grads.1 = (f32[4,96,768]{2,1,0:T(8,128)S(1)}, f32[24,768]{1,0:T(8,128)S(1)}) custom-call(bf16[4,768,3072]{2,1,0:T(8,128)(2,1)} %pad_maximum_fusion.g_ref, f32[24,768]{1,0:T(8,128)S(1)} %pad.13.v_ref), custom_call_target="tpu_custom_call" | custom-call | tf_op jit(solution)/shard_map/scatter_grads/pallas_call | solution.py:398
  (283 shorter events, 109.2 us)
Async XLA Ops:
  0.6 8.6 %copy-start.55 = (f32[2,2,192]{2,1,0:T(2,128)S(1)}, f32[2,2,192]{2,1,0:T(2,128)}, u32[]{:S(2)}) copy-start(f32[2,2,192]{2,1,0:T(2,128)} %param.18) | copy-start | bytes 9220
  0.7 8.7 %copy-start.47 = (bf16[2,192,384]{2,1,0:T(8,128)(2,1)S(1)}, bf16[2,192,384]{2,1,0:T(8,128)(2,1)}, u32[]{:S(2)}) copy-start(bf16[2,192,384]{2,1,0:T(8,128)(2,1)} %param.19) | copy-start | bytes 884740
  2.7 37.9 %copy-start.46 = (bf16[768,384]{1,0:T(8,128)(2,1)S(1)}, bf16[768,384]{1,0:T(8,128)(2,1)}, u32[]{:S(2)}) copy-start(bf16[768,384]{1,0:T(8,128)(2,1)} %param.23) | copy-start | bytes 1769476
  2.7 164.9 %all-to-all-start = ((bf16[2,4,49,768]{3,2,0,1:T(8,128)(2,1)}), bf16[2,4,49,768]{3,2,0,1:T(8,128)(2,1)S(1)}, u32[]{:S(2)}, u32[]{:S(2)}) async-start(bf16[2,4,49,768]{3,2,0,1:T(8,128)(2,1)} %copy.755), calls=%async_computation | async-start | bytes 1376256 | tf_op jit(solution)/shard_map/all_to_all | solution.py:499
  145.6 7.0 %copy-start.54 = (f32[2,768]{1,0:T(2,128)S(1)}, f32[2,768]{1,0:T(2,128)}, u32[]{:S(2)}) copy-start(f32[2,768]{1,0:T(2,128)} %param.20) | copy-start | bytes 18436
  145.6 7.0 %copy-start.52 = (f32[3,768]{1,0:T(4,128)S(1)}, f32[3,768]{1,0:T(4,128)}, u32[]{:S(2)}) copy-start(f32[3,768]{1,0:T(4,128)} %param.16) | copy-start | bytes 27652
  145.6 7.0 %copy-start.53 = (f32[3,768]{1,0:T(4,128)S(1)}, f32[3,768]{1,0:T(4,128)}, u32[]{:S(2)}) copy-start(f32[3,768]{1,0:T(4,128)} %param.15) | copy-start | bytes 27652
  152.7 15.5 %copy-start.48 = (f32[768]{0:T(1024)}, f32[768]{0:T(1024)S(1)}, u32[]{:S(2)}) copy-start(f32[768]{0:T(1024)S(1)} %get-tuple-element.192) | copy-start | bytes 9220
  167.6 5.1 copy-start.16
  176.6 17.2 %copy-start.25 = (bf16[2,196,768]{1,2,0:T(8,128)(2,1)}, bf16[2,196,768]{1,2,0:T(8,128)(2,1)S(1)}, u32[]{:S(2)}) copy-start(bf16[2,196,768]{1,2,0:T(8,128)(2,1)S(1)} %copy.765) | copy-start | bytes 1806340
  200.3 5.5 copy-start.45
  201.6 21.2 %all-to-all-start.1 = ((bf16[2,1,196,768]{3,0,1,2:T(2,128)(2,1)}), bf16[2,1,196,768]{3,0,1,2:T(2,128)(2,1)S(1)}, u32[]{:S(2)}, u32[]{:S(2)}) async-start(bf16[2,1,196,768]{3,0,1,2:T(2,128)(2,1)} %copy.780), calls=%async_computation.1 | async-start | bytes 1204224 | tf_op jit(solution)/shard_map/all_to_all | solution.py:502
  222.8 13.2 %all-to-all-start.4 = ((bf16[4,100,768]{2,0,1:T(4,128)(2,1)}), bf16[4,100,768]{2,0,1:T(4,128)(2,1)S(1)}, u32[]{:S(2)}, u32[]{:S(2)}) async-start(bf16[4,100,768]{2,0,1:T(4,128)(2,1)} %pad.12), calls=%async_computation.4 | async-start | bytes 1228800 | tf_op jit(solution)/shard_map/all_to_all | solution.py:507
  226.3 6.7 %copy-start.56 = (s32[2]{0:T(128)S(1)}, s32[2]{0:T(128)}, u32[]{:S(2)}) copy-start(s32[2]{0:T(128)} %constant.122) | copy-start | bytes 28
  236.0 13.2 %all-to-all-start.2 = ((bf16[4,100,768]{2,0,1:T(4,128)(2,1)}), bf16[4,100,768]{2,0,1:T(4,128)(2,1)S(1)}, u32[]{:S(2)}, u32[]{:S(2)}) async-start(bf16[4,100,768]{2,0,1:T(4,128)(2,1)} %pad.11), calls=%async_computation.2 | async-start | bytes 1228800 | tf_op jit(solution)/shard_map/all_to_all | solution.py:507
  251.6 4.6 copy-start.40
  274.4 3.2 copy-start.50
  277.2 42.2 %copy-start.12 = (f32[16,25,768]{2,1,0:T(8,128)}, f32[16,25,768]{2,1,0:T(8,128)S(1)}, u32[]{:S(2)}) copy-start(f32[16,25,768]{2,1,0:T(8,128)S(1)} %get-tuple-element.172) | copy-start | bytes 3686404
  277.6 22.5 %slice-start.2 = ((s8[18874368]{0:T(1024)(128)(4,1)}), s8[4194304]{0:T(1024)(128)(4,1)S(1)}, s32[]{:S(2)}) async-start(s8[18874368]{0:T(1024)(128)(4,1)} %bitcast.287), calls=%async_computation.10 | async-start | bytes 8388608
  277.6 22.4 %slice-start.3 = ((s8[18874368]{0:T(1024)(128)(4,1)}), s8[4194304]{0:T(1024)(128)(4,1)S(1)}, s32[]{:S(2)}) async-start(s8[18874368]{0:T(1024)(128)(4,1)} %bitcast.287), calls=%async_computation.11 | async-start | bytes 8388608
  277.6 22.4 %slice-start.4 = ((s8[18874368]{0:T(1024)(128)(4,1)}), s8[4194304]{0:T(1024)(128)(4,1)S(1)}, s32[]{:S(2)}) async-start(s8[18874368]{0:T(1024)(128)(4,1)} %bitcast.287), calls=%async_computation.12 | async-start | bytes 8388608
  277.6 22.4 %slice-start.5 = ((s8[18874368]{0:T(1024)(128)(4,1)}), s8[4194304]{0:T(1024)(128)(4,1)S(1)}, s32[]{:S(2)}) async-start(s8[18874368]{0:T(1024)(128)(4,1)} %bitcast.287), calls=%async_computation.13 | async-start | bytes 8388608
  284.6 15.5 %copy-start.11 = (f32[16,25,3072]{2,1,0:T(8,128)}, f32[16,25,3072]{2,1,0:T(8,128)S(1)}, u32[]{:S(2)}) copy-start(f32[16,25,3072]{2,1,0:T(8,128)S(1)} %get-tuple-element.173) | copy-start | bytes 14745604
  284.6 15.5 %slice-start.6 = ((s8[18874368]{0:T(1024)(128)(4,1)}), s8[2097152]{0:T(1024)(128)(4,1)S(1)}, s32[]{:S(2)}) async-start(s8[18874368]{0:T(1024)(128)(4,1)} %bitcast.287), calls=%async_computation.14 | async-start | bytes 4194304
  284.6 15.5 %copy-start.9 = (bf16[4,4,25,768]{3,2,1,0:T(8,128)(2,1)S(1)}, bf16[4,4,25,768]{3,2,1,0:T(8,128)(2,1)}, u32[]{:S(2)}) copy-start(bf16[4,4,25,768]{3,2,1,0:T(8,128)(2,1)} %copy.806) | copy-start | bytes 1843204
  309.1 5.1 copy-start.58
  320.1 2.9 copy-start.4
  320.5 2.6 copy-start.39
  327.3 3.6 copy-start.8
  339.9 3.5 copy-start.10
  343.4 6.7 %copy-start.27 = (bf16[16,25,12,64]{3,0,1,2:T(8,128)(2,1)S(1)}, bf16[16,25,12,64]{3,0,1,2:T(8,128)(2,1)}, u32[]{:S(2)}) copy-start(bf16[16,25,12,64]{3,0,1,2:T(8,128)(2,1)} %get-tuple-element.184) | copy-start | bytes 1843204
  351.7 3.4 copy-start.30
  355.1 3.2 copy-start.14
  359.9 3.4 copy-start.1
  368.3 5.1 copy-start.57
  370.0 15.1 %all-to-all-start.5 = ((bf16[16,25,768]{2,1,0:T(8,128)(2,1)}), bf16[16,25,768]{2,1,0:T(8,128)(2,1)S(1)}, u32[]{:S(2)}, u32[]{:S(2)}) async-start(bf16[16,25,768]{2,1,0:T(8,128)(2,1)} %add_convert_fusion.1), calls=%async_computation.5 | async-start | bytes 1572864 | tf_op jit(solution)/shard_map/all_to_all | solution.py:510
  385.0 15.1 %all-to-all-start.3 = ((bf16[16,25,768]{2,1,0:T(8,128)(2,1)}), bf16[16,25,768]{2,1,0:T(8,128)(2,1)S(1)}, u32[]{:S(2)}, u32[]{:S(2)}) async-start(bf16[16,25,768]{2,1,0:T(8,128)(2,1)} %add_convert_fusion.2), calls=%async_computation.3 | async-start | bytes 1572864 | tf_op jit(solution)/shard_map/all_to_all | solution.py:510
  388.5 3.2 copy-start.41
  388.6 3.2 copy-start.42
  394.2 9.4 %copy-start.21 = (bf16[16,25,768]{2,0,1:T(8,128)(2,1)S(1)}, bf16[16,25,768]{2,0,1:T(8,128)(2,1)}, u32[]{:S(2)}) copy-start(bf16[16,25,768]{2,0,1:T(8,128)(2,1)} %reshape.428) | copy-start | bytes 1843204
  400.1 20.8 %all-to-all-start.6 = ((bf16[2,4,49,768]{3,0,2,1:T(2,128)(2,1)}), bf16[2,4,49,768]{3,0,2,1:T(2,128)(2,1)S(1)}, u32[]{:S(2)}, u32[]{:S(2)}) async-start(bf16[2,4,49,768]{3,0,2,1:T(2,128)(2,1)} %copy.825), calls=%async_computation.6 | async-start | bytes 1204224 | tf_op jit(solution)/shard_map/all_to_all | solution.py:499
  425.1 8.4 %slice-start = ((s8[4915200]{0:T(1024)(128)(4,1)}), s8[4194304]{0:T(1024)(128)(4,1)S(1)}, s32[]{:S(2)}) async-start(s8[4915200]{0:T(1024)(128)(4,1)} %bitcast.285), calls=%async_computation.8 | async-start | bytes 8388608
  429.7 3.9 slice-start.1
  441.9 3.1 copy-start.38
  445.1 3.1 copy-start.20
  452.0 6.3 %copy-start.33 = (bf16[768,768]{0,1:T(8,128)(2,1)S(1)}, bf16[768,768]{0,1:T(8,128)(2,1)}, u32[]{:S(2)}) copy-start(bf16[768,768]{0,1:T(8,128)(2,1)} %bitcast_convert_fusion.2) | copy-start | bytes 3538948
  453.3 138.3 %all-to-all-start.7 = ((bf16[2,1,196,768]{3,0,1,2:T(2,128)(2,1)}), bf16[2,1,196,768]{3,0,1,2:T(2,128)(2,1)S(1)}, u32[]{:S(2)}, u32[]{:S(2)}) async-start(bf16[2,1,196,768]{3,0,1,2:T(2,128)(2,1)} %copy.850), calls=%async_computation.7 | async-start | bytes 1204224 | tf_op jit(solution)/shard_map/all_to_all | solution.py:502
  462.2 6.7 %copy-start.51 = (f32[1,768]{1,0:T(1,128)S(1)}, f32[1,768]{1,0:T(1,128)}, u32[]{:S(2)}) copy-start(f32[1,768]{1,0:T(1,128)} %reshape.438) | copy-start | bytes 9220
  (26 other events, 43.6 us)

commit v3 on v2

--- a/solution.py
+++ b/solution.py
@@ -50,7 +50,7 @@
         pl.when(when)(action)
 
 
-def gather_kernel(shard, whole, send_sem, recv_sem, local_sem):
+def gather_kernel(shard, bias, whole, bias_all, send_sem, recv_sem, local_sem, bias_send, bias_recv):
     x, c, z = lax.axis_index("fsdp"), lax.axis_index("ctx"), lax.axis_index("tp")
     y, k = c // 2, c % 2
     rows = shard.shape[1] // 4
@@ -62,7 +62,24 @@
         row = pl.multiple_of((f * 4 + cc) * rows, 16)
         return ref.at[piece, pl.ds(row, rows), pl.ds(pl.multiple_of(t * width, 128), width)]
 
-    meet(places, ("x", "y", "core"), z, last)
+    line = [(x, c, (z + i) % 4) for i in range(1, 4)]
+    barrier = pltpu.get_barrier_semaphore()
+    for place in [places[side] for side in ("x", "y", "core")] + line:
+        pl.semaphore_signal(barrier, inc=1, device_id=place, device_id_type=MESH)
+    pl.semaphore_wait(barrier, 6)
+    small = []
+    for i, place in enumerate(line):
+        copy = pltpu.make_async_remote_copy(
+            src_ref=bias,
+            dst_ref=bias_all.at[z],
+            send_sem=bias_send.at[i],
+            recv_sem=bias_recv.at[i],
+            device_id=place,
+            device_id_type=MESH,
+        )
+        copy.start()
+        small.append(copy)
+    bias_all[z] = bias[...]
     local = []
     for piece in range(PIECES):
         row = pl.multiple_of(x * rows * 4, 16)
@@ -180,38 +197,43 @@
                 copy.wait_send()
 
         maybe(when, wait)
-    for copy in local:
+    for copy in local + small:
         copy.wait()
 
 
-def gather(shard):
+def gather(shard, bias):
     ranks = (lax.axis_size("fsdp"), lax.axis_size("ctx"), lax.axis_size("tp"))
     rows, width = shard.shape[1:]
     if ranks != (2, 4, 4):
         part = rows // ranks[1]
         mine = lax.dynamic_slice_in_dim(shard, lax.axis_index("ctx") * part, part, 1)
         tall = lax.all_gather(mine, ("fsdp", "ctx"), axis=1, tiled=True)
-        return lax.all_gather(tall, "tp", axis=2, tiled=True)
+        return lax.all_gather(tall, "tp", axis=2, tiled=True), lax.all_gather(bias, "tp")
     return pl.pallas_call(
         gather_kernel,
-        out_shape=jax.ShapeDtypeStruct((PIECES, rows * 2, width * 4), BF),
-        in_specs=[pl.BlockSpec(memory_space=pltpu.VMEM)],
-        out_specs=pl.BlockSpec(memory_space=pl.ANY),
+        out_shape=(
+            jax.ShapeDtypeStruct((PIECES, rows * 2, width * 4), BF),
+            jax.ShapeDtypeStruct((4,) + bias.shape, F32),
+        ),
+        in_specs=[pl.BlockSpec(memory_space=pltpu.VMEM)] * 2,
+        out_specs=[pl.BlockSpec(memory_space=pl.ANY), pl.BlockSpec(memory_space=pltpu.VMEM)],
         scratch_shapes=[
             pltpu.SemaphoreType.DMA((260,)),
             pltpu.SemaphoreType.DMA((32, PIECES)),
             pltpu.SemaphoreType.DMA((PIECES,)),
+            pltpu.SemaphoreType.DMA((3,)),
+            pltpu.SemaphoreType.DMA((3,)),
         ],
         compiler_params=pltpu.CompilerParams(collective_id=0, has_side_effects=True),
         name="gather_weights",
-    )(shard)
+    )(shard, bias)
 
 
 STEPS = 16
 
 
 def scatter_kernel(
-    g_ref, v_ref, out_ref, vout_ref, own, r1, r2, r3x, r3y, rup, rdn, vr, va,
+    g0, g1, g2, g3, v_ref, out_ref, vout_ref, own, r1, r2, r3x, r3y, rup, rdn, vr, va,
     own_sem, s1, q1, s2, q2, s3a, s3b, q3x, q3y, sz, qup, qdn, vs, vq,
 ):
     x, c, z = lax.axis_index("fsdp"), lax.axis_index("ctx"), lax.axis_index("tp")
@@ -224,10 +246,12 @@
     def tp_of(s):
         return (3 * s) % 4
 
-    def spot(f, yy, kk, s):
+    pieces = (g0, g1, g2, g3)
+
+    def spot(f, yy, kk, s, piece=0):
         row = pl.multiple_of((f * 4 + yy * 2 + kk) * rows, 16)
         column = pl.multiple_of(tp_of(s) * width, 128)
-        return g_ref.at[s // 4, pl.ds(row, rows), pl.ds(column, width)]
+        return pieces[piece].at[0, pl.ds(row, rows), pl.ds(column, width)]
 
     def remote(src, dst, send, recv, side):
         return pltpu.make_async_remote_copy(
@@ -235,13 +259,13 @@
             device_id=places[side], device_id_type=MESH,
         )
 
-    def core_copy(s, f, yy):
+    def core_copy(s, f, yy, piece=0):
         return remote(
-            spot(f, yy, 1 - k, s), r1.at[s, f, yy], s1.at[s, f, yy], q1.at[s, f, yy], "core"
+            spot(f, yy, 1 - k, s, piece), r1.at[s, f, yy], s1.at[s, f, yy], q1.at[s, f, yy], "core"
         )
 
-    def own_copy(s, f, yy):
-        return pltpu.make_async_copy(spot(f, yy, k, s), own.at[s, f, yy], own_sem.at[s, f, yy])
+    def own_copy(s, f, yy, piece=0):
+        return pltpu.make_async_copy(spot(f, yy, k, s, piece), own.at[s, f, yy], own_sem.at[s, f, yy])
 
     def diag_copy(s, side):
         return remote(r1.at[s, 1 - x, 1 - y], r2.at[s], s2.at[s], q2.at[s], side)
@@ -265,13 +289,15 @@
 
     quads = [(f, yy) for f in range(2) for yy in range(2)]
 
-    def start(s, carry):
-        for f, yy in quads:
-            core_copy(s, f, yy).start()
-            own_copy(s, f, yy).start()
-        return carry
-
-    lax.fori_loop(0, STEPS, start, 0)
+    for piece in range(PIECES):
+
+        def start(s, carry):
+            for f, yy in quads:
+                core_copy(s, f, yy, piece).start()
+                own_copy(s, f, yy, piece).start()
+            return carry
+
+        lax.fori_loop(piece * 4, piece * 4 + 4, start, 0)
     va[0] = v_ref[...]
     v_copy(0).start()
 
@@ -387,10 +413,10 @@
 
 def scatter(grads, vectors):
     ranks = (lax.axis_size("fsdp"), lax.axis_size("ctx"), lax.axis_size("tp"))
-    rows = grads.shape[1] // (ranks[0] * ranks[1])
-    width = grads.shape[2] // ranks[2]
+    rows = grads[0].shape[1] // (ranks[0] * ranks[1])
+    width = grads[0].shape[2] // ranks[2]
     if ranks != (2, 4, 4):
-        tall = lax.psum_scatter(grads, ("fsdp", "ctx"), scatter_dimension=1, tiled=True)
+        tall = lax.psum_scatter(jnp.concatenate(grads), ("fsdp", "ctx"), scatter_dimension=1, tiled=True)
         own = lax.psum_scatter(tall, "tp", scatter_dimension=2, tiled=True)
         return own.astype(F32), lax.psum(vectors, ALL)
     sub = (rows, width)
@@ -401,7 +427,7 @@
             jax.ShapeDtypeStruct((PIECES,) + sub, F32),
             jax.ShapeDtypeStruct(vectors.shape, F32),
         ),
-        in_specs=[pl.BlockSpec(memory_space=pl.ANY), pl.BlockSpec(memory_space=pltpu.VMEM)],
+        in_specs=[pl.BlockSpec(memory_space=pl.ANY)] * 4 + [pl.BlockSpec(memory_space=pltpu.VMEM)],
         out_specs=[pl.BlockSpec(memory_space=pltpu.VMEM)] * 2,
         scratch_shapes=[pltpu.VMEM((STEPS, 2, 2) + sub, BF)] * 2
         + [pltpu.VMEM((STEPS,) + sub, BF)] * 5
@@ -413,40 +439,324 @@
             collective_id=1, has_side_effects=True, vmem_limit_bytes=48 * 2**20
         ),
         name="scatter_grads",
-    )(grads, vectors)
-
-
-def layer_norm(rows, gain, shift):
+    )(*grads, vectors)
+
+
+def nn(a, b):
+    return lax.dot_general(a, b, (((1,), (0,)), ((), ())), preferred_element_type=F32)
+
+
+def nt(a, b):
+    return lax.dot_general(a, b, (((1,), (1,)), ((), ())), preferred_element_type=F32)
+
+
+def tn(a, b):
+    return lax.dot_general(a, b, (((0,), (0,)), ((), ())), preferred_element_type=F32)
+
+
+def normalise(rows):
     centre = rows - jnp.mean(rows, axis=-1, keepdims=True)
-    spread = jnp.mean(centre * centre, axis=-1, keepdims=True)
-    return centre * lax.rsqrt(spread + EPSILON) * gain + shift
-
-
-def gelu_exact(values):
-    return jax.nn.gelu(values, approximate=False)
-
-
-def dot(form, a, b):
-    return jnp.einsum(form, a, b, preferred_element_type=F32)
-
-
-def attend(q, k, v):
-    scores = dot("hgqe,hgke->hgqk", q, k) * 0.125
-    highest = jnp.max(scores, axis=-1, keepdims=True)
-    log_total = highest + jnp.log(jnp.sum(jnp.exp(scores - highest), axis=-1, keepdims=True))
-    weights = jnp.exp(scores - log_total).astype(BF)
-    return dot("hgqk,hgke->hgqe", weights, v).astype(BF), log_total
-
-
-def attend_back(q, k, v, log_total, grad):
-    probs = jnp.exp(dot("hgqe,hgke->hgqk", q, k) * 0.125 - log_total)
-    grad_probs = dot("hgqe,hgke->hgqk", grad, v)
-    inner = jnp.sum(probs * grad_probs, axis=-1, keepdims=True)
-    grad_scores = (probs * (grad_probs - inner)).astype(BF)
-    grad_q = dot("hgqk,hgke->hgqe", grad_scores, k) * 0.125
-    grad_k = dot("hgqk,hgqe->hgke", grad_scores, q) * 0.125
-    grad_v = dot("hgqk,hgqe->hgke", probs.astype(BF), grad)
-    return jnp.stack([grad_q, grad_k, grad_v]).astype(BF)
+    scale = lax.rsqrt(jnp.mean(centre * centre, axis=-1, keepdims=True) + EPSILON)
+    return centre * scale, scale
+
+
+def norm_back(rows, gain, grad):
+    unit, scale = normalise(rows)
+    inner = grad * gain
+    mean = jnp.mean(inner, axis=-1, keepdims=True)
+    along = jnp.mean(inner * unit, axis=-1, keepdims=True)
+    return scale * (inner - mean - unit * along), jnp.sum(grad * unit, axis=0, keepdims=True), jnp.sum(
+        grad, axis=0, keepdims=True
+    )
+
+
+def lanes_in(low, high):
+    lane = lax.broadcasted_iota(jnp.int32, (1, 256), 1)
+    return jnp.where((lane >= low) & (lane < high), 1.0, 0.0)
+
+
+def stack_heads(values):
+    return jnp.concatenate(
+        [values * lanes_in(i * HEAD, i * HEAD + HEAD).astype(BF) for i in range(3)], axis=0
+    )
+
+
+def pick_heads(stacked):
+    rows = stacked.shape[0] // 3
+    return sum(
+        stacked[i * rows : (i + 1) * rows] * lanes_in(i * HEAD, i * HEAD + HEAD) for i in range(3)
+    )
+
+
+def shifted(values):
+    return pltpu.roll(values, 64, axis=1)
+
+
+def unshifted(values):
+    return pltpu.roll(values, 192, axis=1)
+
+
+def block(w_ref, t, start, size):
+    return w_ref[:, pl.ds(pl.multiple_of(t * (w_ref.shape[1] // 4) + start, 128), size)]
+
+
+class Attention:
+    def __init__(self, groups, rows, penalty, w, bias, q, k, v, o, p):
+        self.groups, self.rows, self.penalty = groups, rows, penalty
+        self.w, self.bias, self.q, self.k, self.v, self.o, self.p = w, bias, q, k, v, o, p
+
+    def spans(self):
+        return [(g, pl.ds(g * self.rows, self.rows)) for g in range(self.groups)]
+
+    def forward(self, normed, total):
+        used = lanes_in(0, 192)
+
+        def body(t, carry):
+            mixed = nn(normed[...], block(self.w, t, 0, 640))
+            self.q[t] = ((mixed[:, :256] + self.bias[t, 0:1]) * used).astype(BF)
+            self.k[t] = (unshifted(mixed[:, 128:384]) * used).astype(BF)
+            self.v[t] = ((mixed[:, 384:] + self.bias[t, 1:2]) * used).astype(BF)
+            for g, span in self.spans():
+                scores = nt(stack_heads(self.q[t, span]), self.k[t, span]) * 0.125 + self.penalty()
+                weights = jnp.exp(scores - jnp.max(scores, axis=-1, keepdims=True))
+                weights = weights * (1.0 / jnp.sum(weights, axis=-1, keepdims=True))
+                weights = weights.astype(BF)
+                self.p[t, g] = weights
+                out = pick_heads(nn(weights, self.v[t, span]))
+                self.o[t, span] = shifted(out).astype(BF)
+            total[...] += nt(self.o[t], block(self.w, t, 512, 256))
+            return carry
+
+        lax.fori_loop(0, 4, body, 0)
+
+    def backward(self, normed_t, branch, branch_t, dk, dv, grad_normed, grad_w, grad_bias):
+        used = lanes_in(0, 192)
+
+        def body(t, carry):
+            grad_o = (unshifted(nn(branch[...], block(self.w, t, 512, 256))) * used).astype(BF)
+            dq = []
+            for g, span in self.spans():
+                stacked = stack_heads(grad_o[g * self.rows : (g + 1) * self.rows])
+                weights = self.p[t, g]
+                probs = weights.astype(F32)
+                grad_p = nt(stacked, self.v[t, span])
+                inner = jnp.sum(probs * grad_p, axis=-1, keepdims=True)
+                grad_s = (probs * (grad_p - inner)).astype(BF)
+                dq.append((pick_heads(nn(grad_s, self.k[t, span])) * 0.125).astype(BF))
+                dk[span] = shifted(tn(grad_s, stack_heads(self.q[t, span])) * 0.125).astype(BF)
+                dv[span] = tn(weights, stacked).astype(BF)
+            dq = jnp.concatenate(dq, axis=0)
+            grad_normed[...] += (
+                nt(dq, block(self.w, t, 0, 256))
+                + nt(dk[...], block(self.w, t, 128, 256))
+                + nt(dv[...], block(self.w, t, 384, 256))
+            )
+            for start, low, high in (
+                (0, nn(normed_t[...], dq), nn(normed_t[...], dk[...])),
+                (384, nn(normed_t[...], dv[...]), nn(branch_t[...], self.o[t])),
+            ):
+                columns = pl.multiple_of(t * (self.w.shape[1] // 4) + start, 128)
+                grad_w[:, pl.ds(columns, 128)] = low[:, :128].astype(BF)
+                grad_w[:, pl.ds(columns + 128, 128)] = (low[:, 128:] + high[:, :128]).astype(BF)
+                grad_w[:, pl.ds(columns + 256, 128)] = high[:, 128:].astype(BF)
+            grad_bias[t, 0:1] = jnp.sum(dq.astype(F32), axis=0, keepdims=True)
+            grad_bias[t, 1:2] = jnp.sum(dv[...].astype(F32), axis=0, keepdims=True)
+            return carry
+
+        lax.fori_loop(0, 4, body, 0)
+
+
+SP = 208
+
+
+def spatial_penalty(places):
+    def penalty():
+        lane = lax.broadcasted_iota(jnp.int32, (1, SP), 1)
+        return jnp.where(lane < places, 0.0, -1e30)
+    return penalty
+
+
+def spatial_forward_kernel(x_ref, w_ref, bias_ref, norm_ref, ob_ref, h_out, q, k, v, o, p, total, normed):
+    clips, places, model = x_ref.shape
+    for g in range(clips):
+        total[pl.ds(g * SP, places)] = x_ref[g].astype(F32)
+        total[pl.ds(g * SP + places, SP - places)] = jnp.zeros((SP - places, model), F32)
+        span = pl.ds(g * SP, SP)
+        unit, _ = normalise(total[span])
+        normed[span] = (unit * norm_ref[0:1] + norm_ref[1:2]).astype(BF)
+        total[span] += ob_ref[...]
+    att = Attention(clips, SP, spatial_penalty(places), w_ref.at[0], bias_ref, q, k, v, o, p)
+    att.forward(normed, total)
+    for g in range(clips):
+        h_out[g] = total[pl.ds(g * SP, places)].astype(BF)
+
+
+def spatial_back_kernel(x_ref, g_ref, w_ref, norm_ref, q, k, v, o, p,
+                        gx_out, gw, gbias, gvec, total, normed_t, branch, branch_t, dk, dv, gn, rows_in):
+    clips, places, model = x_ref.shape
+    for g in range(clips):
+        for ref, source in ((rows_in, x_ref), (total, g_ref)):
+            ref[pl.ds(g * SP, places)] = source[g].astype(F32)
+            ref[pl.ds(g * SP + places, SP - places)] = jnp.zeros((SP - places, model), F32)
+    attention_back(Attention(clips, SP, None, w_ref.at[0], None, q, k, v, o, p),
+                   rows_in, total, norm_ref, normed_t, branch, branch_t, dk, dv, gn, gw.at[0], gbias, gvec)
+    for g in range(clips):
+        gx_out[g] = total[pl.ds(g * SP, places)].astype(BF)
+
+
+def attention_back(att, rows_in, total, norm_ref, normed_t, branch, branch_t, dk, dv, gn, gw, gbias, gvec):
+    rounded = total[...].astype(BF)
+    branch[...] = rounded
+    branch_t[...] = total[...].T.astype(BF)
+    gvec[2:3] = jnp.sum(rounded.astype(F32), axis=0, keepdims=True)
+    unit, _ = normalise(rows_in[...])
+    normed_t[...] = (unit * norm_ref[0:1] + norm_ref[1:2]).T.astype(BF)
+    gn[...] = jnp.zeros_like(gn)
+    att.backward(normed_t, branch, branch_t, dk, dv, gn, gw, gbias)
+    grad, gain, shift = norm_back(rows_in[...], norm_ref[0:1], gn[...])
+    total[...] += grad
+    gvec[0:1] = gain
+    gvec[1:2] = shift
+
+
+def by_pair(source, target, mix):
+    frames, pairs, model = source.shape
+    for f in range(frames):
+        values = source[f].astype(F32)
+        for i in range(model // 128):
+            mix[i, pl.ds(f, pairs, stride=frames)] = values[:, i * 128 : i * 128 + 128]
+    for i in range(model // 128):
+        target[:, i * 128 : i * 128 + 128] = mix[i]
+
+
+def by_frame(source, target, mix):
+    frames, pairs, model = target.shape
+    for i in range(model // 128):
+        mix[i] = source[:, i * 128 : i * 128 + 128]
+    for f in range(frames):
+        for i in range(model // 128):
+            target[f, :, i * 128 : i * 128 + 128] = mix[i, pl.ds(f, pairs, stride=frames)].astype(BF)
+
+
+TG = 5
+
+
+def temporal_kernel(h_ref, g_ref, w_ref, u_ref, d_ref, bias_ref, norm_ref, norm2_ref, ob_ref, ub_ref, db_ref, pen_ref,
+                    y_out, g_out, gw, gu, gd, gbias, gvec, gvec2, gub,
+                    q, k, v, o, p, rows_in, total, third, grad, normed, normed_t, branch, branch_t, dk, dv, gn, mix):
+    frames, pairs, model = h_ref.shape
+    rows = frames * pairs
+    by_pair(h_ref, rows_in, mix)
+    by_pair(g_ref, grad, mix)
+    unit, _ = normalise(rows_in[...])
+    normed[...] = (unit * norm_ref[0:1] + norm_ref[1:2]).astype(BF)
+    third[...] = rows_in[...] + ob_ref[...]
+    group = TG * frames
+    att = Attention(pairs // TG, group, lambda: pen_ref[...], w_ref.at[0], bias_ref, q, k, v, o, p)
+    att.forward(normed, third)
+    unit, _ = normalise(third[...])
+    n2 = unit * norm2_ref[0:1] + norm2_ref[1:2]
+    normed[...] = n2.astype(BF)
+    normed_t[...] = n2.T.astype(BF)
+    branch[...] = grad[...].astype(BF)
+    branch_t[...] = grad[...].T.astype(BF)
+    gvec2[2:3] = jnp.sum(grad[...], axis=0, keepdims=True)
+    total[...] = third[...] + db_ref[...]
+    gn[...] = jnp.zeros_like(gn)
+    size = 384
+    def mlp(j, carry):
+        columns = pl.ds(pl.multiple_of(j * size, 128), size)
+        up = u_ref[0, :, columns]
+        down = d_ref[0, :, columns]
+        hidden = nn(normed[...], up) + ub_ref[j]
+        half = 0.5 + 0.5 * lax.erf(hidden * (2.0 ** -0.5))
+        active = (hidden * half).astype(BF)
+        slope = half + hidden * (jnp.exp(-0.5 * hidden * hidden) * ((2.0 * jnp.pi) ** -0.5))
+        grad_hidden = nn(branch[...], down) * slope
+        rounded = grad_hidden.astype(BF)
+        gub[j] = jnp.sum(rounded.astype(F32), axis=0, keepdims=True)
+        total[...] += nt(active, down)
+        gn[...] += nt(rounded, up)
+        gd[0, :, columns] = nn(branch_t[...], active).astype(BF)
+        gu[0, :, columns] = nn(normed_t[...], rounded).astype(BF)
+        return carry
+    lax.fori_loop(0, u_ref.shape[2] // size, mlp, 0)
+    by_frame(total, y_out, mix)
+    back, gain, shift = norm_back(third[...], norm2_ref[0:1], gn[...])
+    grad[...] += back
+    gvec2[0:1] = gain
+    gvec2[1:2] = shift
+    attention_back(att, rows_in, grad, norm_ref, normed_t, branch, branch_t, dk, dv, gn, gw.at[0], gbias, gvec)
+    by_frame(grad, g_out, mix)
+
+
+def piece_spec(piece, whole):
+    return pl.BlockSpec((1,) + whole.shape[1:], lambda i: (piece, 0, 0))
+
+
+def full_spec(value):
+    return pl.BlockSpec(value.shape, lambda i: (0,) * len(value.shape))
+
+
+def run(kernel, args, specs, outs, scratch, name):
+    return pl.pallas_call(
+        kernel, grid=(1,),
+        out_shape=outs, in_specs=specs, out_specs=[full_spec(out) for out in outs], scratch_shapes=scratch,
+        compiler_params=pltpu.CompilerParams(vmem_limit_bytes=63 * 2**20),
+        name=name,
+    )(*args)
+
+
+def shape(*size, dtype=BF):
+    return jax.ShapeDtypeStruct(size, dtype)
+
+
+def spatial_forward(x, whole, bias, norm, out_bias):
+    clips, places, model = x.shape
+    rows = clips * SP
+    args = (x, whole, bias, norm, out_bias)
+    specs = [full_spec(a) for a in args]
+    specs[1] = piece_spec(0, whole)
+    outs = [shape(clips, places, model)] + [shape(4, rows, 256)] * 4 + [shape(4, clips, 3 * SP, SP)]
+    return run(spatial_forward_kernel, args, specs, outs,
+               [pltpu.VMEM((rows, model), F32), pltpu.VMEM((rows, model), BF)], "spatial_forward")
+
+
+def spatial_back(x, g, whole, norm, kept):
+    clips, places, model = x.shape
+    rows = clips * SP
+    args = (x, g, whole, norm) + tuple(kept)
+    specs = [full_spec(a) for a in args]
+    specs[2] = piece_spec(0, whole)
+    outs = [shape(clips, places, model), shape(1, *whole.shape[1:]), shape(4, 2, 256, dtype=F32), shape(3, model, dtype=F32)]
+    scratch = [pltpu.VMEM((rows, model), F32), pltpu.VMEM((model, rows), BF), pltpu.VMEM((rows, model), BF),
+               pltpu.VMEM((model, rows), BF), pltpu.VMEM((rows, 256), BF), pltpu.VMEM((rows, 256), BF),
+               pltpu.VMEM((rows, model), F32), pltpu.VMEM((rows, model), F32)]
+    return run(spatial_back_kernel, args, specs, outs, scratch, "spatial_back")
+
+
+def temporal(h, g, whole, bias, norm, norm2, out_bias, up_bias, down_bias):
+    frames, pairs, model = h.shape
+    rows = frames * pairs
+    group = TG * frames
+    row = jnp.arange(3 * group)[:, None] % group // frames
+    column = jnp.arange(group)[None] // frames
+    penalty = jnp.where(row == column, 0.0, -1e30).astype(F32)
+    args = (h, g, whole, whole, whole, bias, norm, norm2, out_bias, up_bias.reshape(-1, 1, 384), down_bias, penalty)
+    specs = [full_spec(a) for a in args]
+    for i, piece in ((2, 1), (3, 2), (4, 3)):
+        specs[i] = piece_spec(piece, whole)
+    hidden = whole.shape[2]
+    outs = [shape(frames, pairs, model), shape(frames, pairs, model), shape(1, model, hidden), shape(1, model, hidden),
+            shape(1, model, hidden), shape(4, 2, 256, dtype=F32), shape(3, model, dtype=F32), shape(3, model, dtype=F32),
+            shape(hidden // 384, 1, 384, dtype=F32)]
+    big = pltpu.VMEM((rows, model), F32)
+    low = pltpu.VMEM((rows, model), BF)
+    flip = pltpu.VMEM((model, rows), BF)
+    part = pltpu.VMEM((rows, 256), BF)
+    scratch = [pltpu.VMEM((4, rows, 256), BF)] * 4 + [pltpu.VMEM((4, pairs // TG, 3 * group, group), BF)] + [
+        big, big, big, big, low, flip, low, flip, part, part, big, pltpu.VMEM((model // 128, rows, 128), F32)]
+    return run(temporal_kernel, args, specs, outs, scratch, "temporal_and_mlp")
 
 
 def local(
@@ -463,11 +773,10 @@
     down_weight,
     down_bias,
 ):
-    ranks_c, ranks_t = lax.axis_size("ctx"), lax.axis_size("tp")
+    ranks_c = lax.axis_size("ctx")
     tp_rank = lax.axis_index("tp")
     clips, frames, places, model = inputs.shape
     width = attn_weight.shape[3]
-    heads = model // HEAD
 
     shard = jnp.concatenate(
         [
@@ -482,18 +791,14 @@
             down_weight.T[None],
         ]
     )
-    whole = gather(shard)
-    qkv_full, out_full = [], []
-    for layer in range(2):
-        blocks = whole[layer].reshape(model, ranks_t, 4, width)
-        qkv_full.append([blocks[:, :, j].reshape(model, model) for j in range(3)])
-        out_full.append(blocks[:, :, 3].reshape(model, model))
-    up_full = whole[2]
-    down_full = whole[3]
-    attn_bias_full = lax.all_gather(attn_bias, "tp", axis=2, tiled=True)
+    bias = jnp.pad(attn_bias.reshape(4, width), ((0, 4), (0, 256 - width)))
+    whole, bias = gather(shard, bias)
+    bias = bias[:, :4].reshape(4, 2, 2, 256).transpose(1, 0, 2, 3)
+    norm = jnp.stack([norm_gain, norm_bias], axis=1)
 
     pairs = clips * places
     share = -(-pairs // ranks_c)
+    share += -share % TG
 
     def home_to_spatial(values):
         return lax.all_to_all(values, "tp", split_axis=1, concat_axis=2, tiled=True)
@@ -510,125 +815,42 @@
         rows = lax.all_to_all(values, "ctx", split_axis=0, concat_axis=1, tiled=True)[:, :pairs]
         return rows.reshape(frames, clips, places, model).transpose(1, 0, 2, 3)
 
-    def heads_apart(values, temporal):
-        apart = values.reshape(values.shape[:2] + (heads, HEAD))
-        return apart.transpose(2, 1, 0, 3) if temporal else apart.transpose(2, 0, 1, 3)
-
-    def heads_joined(values, temporal):
-        joined = values.transpose(2, 1, 0, 3) if temporal else values.transpose(1, 2, 0, 3)
-        return joined.reshape(joined.shape[:2] + (model,))
-
-    def attn_forward(stream, index, temporal):
-        normed = layer_norm(stream, norm_gain[index], norm_bias[index]).astype(BF)
-        biases = (attn_bias_full[index, 0], 0.0, attn_bias_full[index, 1])
-        triple = [
-            heads_apart((dot("abd,dc->abc", normed, qkv_full[index][j]) + biases[j]).astype(BF), temporal)
-            for j in range(3)
-        ]
-        mixed, log_total = attend(*triple)
-        mixed = heads_joined(mixed, temporal)
-        stream_next = stream + (dot("abc,dc->abd", mixed, out_full[index]) + out_bias[index])
-        return stream_next, (normed, triple, log_total, mixed)
-
-    def attn_backward(stream, index, kept, grad_stream, temporal):
-        normed, triple, log_total, mixed = kept
-        grad_branch = grad_stream.astype(BF)
-        grad_bias_out = jnp.sum(grad_branch.astype(F32), axis=(0, 1))
-        grad_weight_out = dot("abc,abd->dc", mixed, grad_branch)
-        grad_mixed = dot("abd,dc->abc", grad_branch, out_full[index]).astype(BF)
-        grad_triple = attend_back(*triple, log_total, heads_apart(grad_mixed, temporal))
-        grad_triple = [heads_joined(grad_triple[j], temporal) for j in range(3)]
-        grad_weight_attn = [dot("abd,abc->dc", normed, g) for g in grad_triple]
-        sums = [jnp.sum(g.astype(F32), axis=(0, 1)) for g in grad_triple]
-        grad_normed = sum(
-            dot("abc,dc->abd", grad_triple[j], qkv_full[index][j]) for j in range(3)
-        )
-        unused, pull = jax.vjp(layer_norm, stream, norm_gain[index], norm_bias[index])
-        grad_input, grad_gain, grad_shift = pull(grad_normed)
-        return grad_stream + grad_input, (
-            grad_gain,
-            grad_shift,
-            grad_weight_attn,
-            jnp.stack([sums[0], sums[2]]),
-            grad_weight_out,
-            grad_bias_out,
-        )
-
     first = home_to_spatial(inputs)
     spatial_shape = first.shape
-    first = first.reshape((-1,) + first.shape[2:]).astype(F32)
-    second, kept_spatial = attn_forward(first, 0, False)
-    second = home_to_temporal(
-        spatial_to_home(second.astype(BF).reshape(spatial_shape))
-    ).astype(F32)
-    third, kept_temporal = attn_forward(second, 1, True)
-    normed = layer_norm(third, norm_gain[2], norm_bias[2]).astype(BF)
-    units = dot("abd,dc->abc", normed, up_full) + up_bias
-    active = gelu_exact(units).astype(BF)
-    result = third + (dot("abc,dc->abd", active, down_full) + down_bias)
-    outputs = temporal_to_home(result.astype(BF))
-
+    first = first.reshape((-1,) + first.shape[2:])
+    second, *kept = spatial_forward(first, whole, bias[0], norm[0], out_bias[0:1])
+    second = home_to_temporal(spatial_to_home(second.reshape(spatial_shape)))
     grad_out = home_to_temporal(cotangent)
-    grad_bias_down = jnp.sum(grad_out.astype(F32), axis=(0, 1))
-    grad_weight_down = dot("abc,abd->dc", active, grad_out)
-    grad_active = dot("abd,dc->abc", grad_out, down_full)
-    unused, pull_gelu = jax.vjp(gelu_exact, units)
-    grad_units = pull_gelu(grad_active)[0].astype(BF)
-    grad_bias_up = jnp.sum(grad_units.astype(F32), axis=(0, 1))
-    grad_weight_up = dot("abd,abc->dc", normed, grad_units)
-    grad_normed = dot("abc,dc->abd", grad_units, up_full)
-    unused, pull = jax.vjp(layer_norm, third, norm_gain[2], norm_bias[2])
-    grad_third, gain_mlp, shift_mlp = pull(grad_normed)
-    grad_third = grad_third + grad_out.astype(F32)
-
-    grad_second, temporal_terms = attn_backward(second, 1, kept_temporal, grad_third, True)
-    grad_second = home_to_spatial(temporal_to_home(grad_second.astype(BF)))
-    grad_second = grad_second.reshape(first.shape).astype(F32)
-    grad_first, spatial_terms = attn_backward(first, 0, kept_spatial, grad_second, False)
-    input_grad = spatial_to_home(grad_first.astype(BF).reshape(spatial_shape))
-
-    def joined(terms):
-        parts = [g.astype(BF).reshape(model, ranks_t, width) for g in terms[2] + [terms[4]]]
-        return jnp.stack(parts, axis=2).reshape(model, -1)
-
-    grads = jnp.stack(
-        [
-            grad_weight_up.astype(BF),
-            grad_weight_down.astype(BF),
-            joined(temporal_terms),
-            joined(spatial_terms),
-        ]
+    result, grad_second, grad_attn1, grad_up, grad_down, bias1, vec1, vec2, grad_up_bias = temporal(
+        second, grad_out, whole, bias[1], norm[1], norm[2], out_bias[1:2], up_bias, down_bias[None]
     )
-    parts = [
-        jnp.stack([spatial_terms[0], temporal_terms[0], gain_mlp]),
-        jnp.stack([spatial_terms[1], temporal_terms[1], shift_mlp]),
-        jnp.stack([spatial_terms[3], temporal_terms[3]]),
-        jnp.stack([spatial_terms[5], temporal_terms[5]]),
-        grad_bias_up,
-        grad_bias_down,
-    ]
-    lines = [p.reshape(-1, model) for p in parts]
-    used = sum(line.shape[0] for line in lines)
-    vectors = jnp.pad(jnp.concatenate(lines), ((0, -used % 8), (0, 0)))
-    own, vectors = scatter(grads, vectors)
-    sums, start = [], 0
-    for part, line in zip(parts, lines):
-        sums.append(vectors[start : start + line.shape[0]].reshape(part.shape))
-        start += line.shape[0]
-    attn = own[jnp.array([3, 2])].reshape(2, own.shape[1], 4, width)
+    outputs = temporal_to_home(result)
+    grad_second = home_to_spatial(temporal_to_home(grad_second)).reshape(first.shape)
+    grad_first, grad_attn0, bias0, vec0 = spatial_back(first, grad_second, whole, norm[0], kept)
+    input_grad = spatial_to_home(grad_first.reshape(spatial_shape))
+
+    attn_bias_sums = jnp.stack([bias0, bias1])[..., :width].transpose(0, 2, 1, 3)
+    lines = [vec0, vec1, vec2, grad_up_bias, attn_bias_sums]
+    flat = jnp.concatenate([line.reshape(-1, model) for line in lines])
+    vectors = jnp.pad(flat, ((0, -flat.shape[0] % 8), (0, 0)))
+    own, vectors = scatter([grad_up, grad_down, grad_attn1, grad_attn0], vectors)
+    triples = vectors[:9].reshape(3, 3, model)
+    ups = up_bias.shape[0] // model
+    attn_bias_sums = vectors[9 + ups : 13 + ups].reshape(2, 2, model)
+    attn = jnp.stack([own[3], own[2]]).reshape(2, own.shape[1], 4, width)
     return (
         outputs,
         input_grad,
-        sums[0],
-        sums[1],
+        triples[:, 0],
+        triples[:, 1],
         attn[:, :, :3].transpose(0, 2, 1, 3),
-        lax.dynamic_slice_in_dim(sums[2], tp_rank * width, width, 2),
+        lax.dynamic_slice_in_dim(attn_bias_sums, tp_rank * width, width, 2),
         attn[:, :, 3].transpose(0, 2, 1),
-        sums[3],
+        triples[:2, 2],
         own[0],
-        sums[4],
+        vectors[9 : 9 + ups].reshape(-1),
         own[1].T,
-        sums[5],
+        triples[2, 2],
     )
 
 

time: 598 us -> 426 us (0.71)
  matrix products: 127 us -> 0 us
  Pallas kernels: 191 us -> 283 us
  local copies, waits for them, and re-layouts: 125 us -> 34.4 us
  other arithmetic: 54.8 us -> 4.92 us
  waiting for transfers between devices: 28.9 us -> 55.8 us
  blocking collectives: 31 us -> 15.1 us
    dot_general x42 -> x0, matrix products: 127 us -> none  [dot(): return jnp.einsum(form, a, b, preferred_element_type=F32)]
    pallas_call x1 -> x4, Pallas kernels: 92.3 us -> 184 us  [the longest x1 95.3 us: gather(): pl.pallas_call(gather_kernel, out_shape=(jax.ShapeDtypeStruct((PIECES, ro...]
    slice x12 -> x8, local copies, waits for them, and re-layouts: 43.2 us -> 2 us  [the longest x2 0.77 us: local(): bias = bias[:, :4].reshape(4, 2, 2, 256).transpose(1, 0, 2, 3)]
    all_gather x1 -> x0, blocking collectives: 31 us -> none  [local(): attn_bias_full = lax.all_gather(attn_bias, 'tp', axis=2, tiled=True)]
    another operation x6 -> x1, other arithmetic: 24.1 us -> 0.04 us  [local(): attn = jnp.stack([own[3], own[2]]).reshape(2, own.shape[1], 4, width)]
    convert_element_type x7 -> x0, other arithmetic: 20 us -> none  [the longest x1 15.4 us: local(): active = gelu_exact(units).astype(BF)]
    reshape x17 -> x12, local copies, waits for them, and re-layouts: 27.2 us -> 7.88 us  [the longest x1 2.37 us: local(): second = home_to_temporal(spatial_to_home(second.reshape(spatial_shape)))]
    all_to_all x0 -> x1, blocking collectives: none -> 15.1 us  [temporal_to_home(): lax.all_to_all(values, 'ctx', split_axis=0, concat_axis=1, tiled=True)]
  transfers between devices with their start and end apart: 8 -> 7, of which waited for: 5 -> 5; matrix products, arithmetic and copies ran while one was open for 20% -> 6% of each run, Pallas kernels for 32% -> 46%
where the time goes in v3:
time: 426 us; the launch traced here: 421 us
  Pallas kernels  283 us (66%)
  waiting for transfers between devices  55.8 us (13%)
  local copies, waits for them, and re-layouts  34.4 us (8%)
  starting transfers between devices  27.4 us (6%)
  blocking collectives  15.1 us (4%)
  other arithmetic  4.92 us (1%)
    pallas_call x1, Pallas kernels, scatter(): pl.pallas_call(scatter_kernel, out_shape=(jax.ShapeDtypeStruct((PIECES,)...  98.3 us
    pallas_call x1, Pallas kernels, gather(): pl.pallas_call(gather_kernel, out_shape=(jax.ShapeDtypeStruct((PIECES, ro...  95.3 us
    pallas_call x3, Pallas kernels, run(): pl.pallas_call(kernel, grid=(1,), out_shape=outs, in_specs=specs, out_spe...  89 us
    all_to_all x2, waiting for transfers between devices, spatial_to_home(): return lax.all_to_all(values, 'tp', split_axis=2, concat_axis=1, tiled=True)  16.1 us
    all_to_all x2, waiting for transfers between devices, home_to_temporal(): return lax.all_to_all(rows, 'ctx', split_axis=1, concat_axis=0, tiled=True)  15.6 us
    all_to_all x1, blocking collectives, temporal_to_home(): lax.all_to_all(values, 'ctx', split_axis=0, concat_axis=1, tiled=True)  15.1 us
    all_to_all x2, waiting for transfers between devices, home_to_spatial(): return lax.all_to_all(values, 'tp', split_axis=1, concat_axis=2, tiled=True)  14.5 us
    unnamed x31, local copies, waits for them, and re-layouts  10.3 us
  transfers between devices with their start and end apart: 7, of which 5 were waited for; matrix products, arithmetic and copies ran while one was open for 6% of the time, Pallas kernels for 46%

profile of v3, /device:TPU:0, one launch (start us, length us, event | category | flops | bytes accessed | tf_op | source)
XLA Modules:
  0.0 421.2 jit_solution(14940954072280368889)
XLA Ops:
  0.7 2.1 copy.85
  2.7 6.3 %all-to-all-start = ((bf16[2,4,49,768]{3,2,0,1:T(8,128)(2,1)}), bf16[2,4,49,768]{3,2,0,1:T(8,128)(2,1)S(1)}, u32[]{:S(2)}, u32[]{:S(2)}) async-start(bf16[2,4,49,768]{3,2,0,1:T(8,128)(2,1)} %copy.85), calls=%async_computation | async-start | bytes 1376256 | tf_op jit(solution)/shard_map/all_to_all | solution.py:804
  9.1 1.3 copy.89
  10.4 1.1 copy.87
  11.6 0.6 copy.88
  12.2 0.6 pad.15.bias
  12.9 2.8 pad_maximum_fusion.shard
  15.6 95.3 %gather_weights.1 = (bf16[4,768,3072]{2,1,0:T(8,128)(2,1)}, f32[4,8,256]{2,1,0:T(8,128)}) custom-call(bf16[4,384,768]{2,1,0:T(8,128)(2,1)} %pad_maximum_fusion.shard, f32[8,256]{1,0:T(8,128)} %pad.15.bias), custom_call_target="tpu_custom_call" | custom-call | tf_op jit(solution)/shard_map/gather_weights/pallas_call | solution.py:212
  110.9 0.8 slice.73
  111.7 0.6 fusion.3
  114.0 0.9 copy.92.x_ref
  114.9 12.2 %spatial_forward.1 = (bf16[2,196,768]{2,1,0:T(8,128)(2,1)}, bf16[4,416,256]{2,1,0:T(8,128)(2,1)}, bf16[4,416,256]{2,1,0:T(8,128)(2,1)}, bf16[4,416,256]{2,1,0:T(...) custom-call(bf16[2,196,768]{2,1,0:T(8,128)(2,1)} %copy.92.x_ref, ...), custom_call_target="tpu_custom_call" | custom-call | tf_op jit(solution)/shard_map/spatial_forward/pallas_call | solution.py:702
  127.1 2.4 copy.93
  129.5 3.5 all-to-all-start.1
  133.0 1.1 pad.17
  134.1 16.1 %all-to-all-done.1 = bf16[2,1,196,768]{3,0,1,2:T(2,128)(2,1)S(1)} async-done(((bf16[2,1,196,768]{3,0,1,2:T(2,128)(2,1)}), bf16[2,1,196,768]{3,0,1,2:T(2,128)(2,1)S(1)}, u32[]{:S(2)}, u32[]{:S(2)}) %all-to-all-start.1) | async-done | bytes 602144 | tf_op jit(solution)/shard_map/all_to_all | solution.py:807
  150.2 3.5 all-to-all-start.3
  153.9 1.1 pad.16
  155.0 8.4 %all-to-all-done.3 = bf16[4,100,768]{2,0,1:T(4,128)(2,1)S(1)} async-done(((bf16[4,100,768]{2,0,1:T(4,128)(2,1)}), bf16[4,100,768]{2,0,1:T(4,128)(2,1)S(1)}, u32[]{:S(2)}, u32[]{:S(2)}) %all-to-all-start.3) | async-done | bytes 614432 | tf_op jit(solution)/shard_map/all_to_all | solution.py:812
  163.4 3.7 all-to-all-start.2
  167.7 0.8 compare_select_fusion.pen_ref
  168.4 1.0 copy.96
  169.4 7.2 %all-to-all-done.2 = bf16[4,100,768]{2,0,1:T(4,128)(2,1)S(1)} async-done(((bf16[4,100,768]{2,0,1:T(4,128)(2,1)}), bf16[4,100,768]{2,0,1:T(4,128)(2,1)S(1)}, u32[]{:S(2)}, u32[]{:S(2)}) %all-to-all-start.2) | async-done | bytes 614432 | tf_op jit(solution)/shard_map/all_to_all | solution.py:812
  176.6 1.0 copy.95
  177.6 55.7 %temporal_and_mlp.1 = (bf16[16,25,768]{2,1,0:T(8,128)(2,1)}, bf16[16,25,768]{2,1,0:T(8,128)(2,1)}, bf16[1,768,3072]{2,1,0:T(8,128)(2,1)}, bf16[1,768,3072]{2,1,0...) custom-call(bf16[16,25,768]{2,1,0:T(8,128)(2,1)} %bitcast.83, ...), custom_call_target="tpu_custom_call" | custom-call | tf_op jit(solution)/shard_map/temporal_and_mlp/pallas_call | solution.py:702
  233.4 15.1 %all_to_all.114 = bf16[16,25,768]{2,1,0:T(8,128)(2,1)S(1)} all-to-all(bf16[16,25,768]{2,1,0:T(8,128)(2,1)} %get-tuple-element.39), channel_id=1, replica_groups=mesh['fsdp'=2,'ctx'=4,'tp'=4] {'ctx'}, dimensions={0} | all-to-all | bytes 1228800 | tf_op jit(solution)/shard_map/all_to_all | solution.py:815
  248.5 3.5 all-to-all-start.4
  252.7 1.3 copy.99
  254.0 9.6 %all-to-all-done.4 = bf16[16,25,768]{2,1,0:T(8,128)(2,1)S(1)} async-done(((bf16[16,25,768]{2,1,0:T(8,128)(2,1)}), bf16[16,25,768]{2,1,0:T(8,128)(2,1)S(1)}, u32[]{:S(2)}, u32[]{:S(2)}) %all-to-all-start.4) | async-done | bytes 614432 | tf_op jit(solution)/shard_map/all_to_all | solution.py:815
  263.6 3.5 all-to-all-start.6
  267.6 1.0 slice.103
  268.6 14.5 %all-to-all-done.6 = bf16[2,4,49,768]{3,0,2,1:T(2,128)(2,1)S(1)} async-done(((bf16[2,4,49,768]{3,0,2,1:T(2,128)(2,1)}), bf16[2,4,49,768]{3,0,2,1:T(2,128)(2,1)S(1)}, u32[]{:S(2)}, u32[]{:S(2)}) %all-to-all-start.6) | async-done | bytes 602144 | tf_op jit(solution)/shard_map/all_to_all | solution.py:804
  283.2 0.9 copy.101.g_ref
  284.1 21.1 %spatial_back.1 = (bf16[2,196,768]{2,1,0:T(8,128)(2,1)}, bf16[1,768,3072]{2,1,0:T(8,128)(2,1)}, f32[4,2,256]{2,1,0:T(2,128)}, f32[3,768]{1,0:T(4,128)}) custom-call(bf16[2,196,768]{2,1,0:T(8,128)(2,1)} %copy.92.x_ref, bf16[2,196,768]{2,1,0:T(8,128)(2,1)} %copy.101.g_ref, bf16[4,768,3072]{2,1,0:T(8,128)(2,1)} %get-tuple-element.35.w_ref.u_ref.d_ref, ...), custom_call_target="tpu_custom_call" | custom-call | tf_op jit(solution)/shard_map/spatial_back/pallas_call | solution.py:702
  305.2 2.4 copy.102
  307.5 3.5 all-to-all-start.7
  311.0 0.7 fusion
  311.8 1.0 concatenate.11
  312.8 2.3 copy-done
  315.1 98.3 %scatter_grads.1 = (f32[4,96,768]{2,1,0:T(8,128)S(1)}, f32[24,768]{1,0:T(8,128)S(1)}) custom-call(bf16[1,768,3072]{2,1,0:T(8,128)(2,1)S(1)} %copy-done, bf16[1,768,3072]{2,1,0:T(8,128)(2,1)} %get-tuple-element.47.g1, bf16[1,768,3072]{2,1,0:T(8,128)(2,1)} %get-tuple-element.48.g2, bf16[1,768,3072]{2,1,0:T(8,128)(2,1)} %get-tuple-element.49.g3, ...), custom_call_target="tpu_custom_call" | custom-call | tf_op jit(solution)/shard_map/scatter_grads/pallas_call | solution.py:424
  413.5 0.9 slice_bitcast_fusion
  415.2 0.9 copy.120
  416.2 0.8 copy.113
  417.6 0.6 reshape.194
  418.2 0.7 constant_dynamic-slice_fusion
  418.9 0.6 slice_reduce_fusion
  419.5 0.6 copy_bitcast_fusion.2
  420.1 1.1 copy.109
  (55 shorter events, 5.4 us)
Async XLA Ops:
  0.6 10.9 %copy-start.1 = (bf16[2,3,384,192]{2,3,1,0:T(8,128)(2,1)S(1)}, bf16[2,3,384,192]{2,3,1,0:T(8,128)(2,1)}, u32[]{:S(2)}) copy-start(bf16[2,3,384,192]{2,3,1,0:T(8,128)(2,1)} %param.16) | copy-start | bytes 2654212
  0.7 11.5 %copy-start.11 = (f32[2,2,192]{2,1,0:T(2,128)S(1)}, f32[2,2,192]{2,1,0:T(2,128)}, u32[]{:S(2)}) copy-start(f32[2,2,192]{2,1,0:T(2,128)} %param.17) | copy-start | bytes 9220
  2.7 110.8 %all-to-all-start = ((bf16[2,4,49,768]{3,2,0,1:T(8,128)(2,1)}), bf16[2,4,49,768]{3,2,0,1:T(8,128)(2,1)S(1)}, u32[]{:S(2)}, u32[]{:S(2)}) async-start(bf16[2,4,49,768]{3,2,0,1:T(8,128)(2,1)} %copy.85), calls=%async_computation | async-start | bytes 1376256 | tf_op jit(solution)/shard_map/all_to_all | solution.py:804
  11.5 100.1 %copy-start.6 = (f32[3,768]{1,0:T(4,128)S(1)}, f32[3,768]{1,0:T(4,128)}, u32[]{:S(2)}) copy-start(f32[3,768]{1,0:T(4,128)} %param.15) | copy-start | bytes 27652
  12.2 99.5 %copy-start.7 = (f32[3,768]{1,0:T(4,128)S(1)}, f32[3,768]{1,0:T(4,128)}, u32[]{:S(2)}) copy-start(f32[3,768]{1,0:T(4,128)} %param.14) | copy-start | bytes 27652
  12.2 100.1 %copy-start.9 = (f32[2,768]{1,0:T(2,128)S(1)}, f32[2,768]{1,0:T(2,128)}, u32[]{:S(2)}) copy-start(f32[2,768]{1,0:T(2,128)} %param.19) | copy-start | bytes 18436
  114.9 18.1 %copy-start.2 = (bf16[2,4,49,768]{3,1,2,0:T(4,128)(2,1)S(1)}, bf16[2,4,49,768]{3,1,2,0:T(4,128)(2,1)}, u32[]{:S(2)}) copy-start(bf16[2,4,49,768]{3,1,2,0:T(4,128)(2,1)} %param.13) | copy-start | bytes 1806340
  127.1 40.0 %copy-start.10 = (f32[768]{0:T(1024)S(1)}, f32[768]{0:T(1024)}, u32[]{:S(2)}) copy-start(f32[768]{0:T(1024)} %param.23) | copy-start | bytes 9220
  129.5 20.7 %all-to-all-start.1 = ((bf16[2,1,196,768]{3,0,1,2:T(2,128)(2,1)}), bf16[2,1,196,768]{3,0,1,2:T(2,128)(2,1)S(1)}, u32[]{:S(2)}, u32[]{:S(2)}) async-start(bf16[2,1,196,768]{3,0,1,2:T(2,128)(2,1)} %copy.93), calls=%async_computation.1 | async-start | bytes 1204224 | tf_op jit(solution)/shard_map/all_to_all | solution.py:807
  150.2 13.2 %all-to-all-start.3 = ((bf16[4,100,768]{2,0,1:T(4,128)(2,1)}), bf16[4,100,768]{2,0,1:T(4,128)(2,1)S(1)}, u32[]{:S(2)}, u32[]{:S(2)}) async-start(bf16[4,100,768]{2,0,1:T(4,128)(2,1)} %pad.17), calls=%async_computation.3 | async-start | bytes 1228800 | tf_op jit(solution)/shard_map/all_to_all | solution.py:812
  163.4 13.2 %all-to-all-start.2 = ((bf16[4,100,768]{2,0,1:T(4,128)(2,1)}), bf16[4,100,768]{2,0,1:T(4,128)(2,1)S(1)}, u32[]{:S(2)}, u32[]{:S(2)}) async-start(bf16[4,100,768]{2,0,1:T(4,128)(2,1)} %pad.16), calls=%async_computation.2 | async-start | bytes 1228800 | tf_op jit(solution)/shard_map/all_to_all | solution.py:812
  233.4 33.7 %copy-start.5 = (f32[8,1,384]{2,1,0:T(1,128)S(1)}, f32[8,1,384]{2,1,0:T(1,128)}, u32[]{:S(2)}) copy-start(f32[8,1,384]{2,1,0:T(1,128)} %get-tuple-element.53) | copy-start | bytes 36868
  248.5 15.1 %all-to-all-start.4 = ((bf16[16,25,768]{2,1,0:T(8,128)(2,1)}), bf16[16,25,768]{2,1,0:T(8,128)(2,1)S(1)}, u32[]{:S(2)}, u32[]{:S(2)}) async-start(bf16[16,25,768]{2,1,0:T(8,128)(2,1)} %get-tuple-element.38), calls=%async_computation.4 | async-start | bytes 1572864 | tf_op jit(solution)/shard_map/all_to_all | solution.py:815
  263.6 19.6 %all-to-all-start.6 = ((bf16[2,4,49,768]{3,0,2,1:T(2,128)(2,1)}), bf16[2,4,49,768]{3,0,2,1:T(2,128)(2,1)S(1)}, u32[]{:S(2)}, u32[]{:S(2)}) async-start(bf16[2,4,49,768]{3,0,2,1:T(2,128)(2,1)} %copy.99), calls=%async_computation.6 | async-start | bytes 1204224 | tf_op jit(solution)/shard_map/all_to_all | solution.py:804
  284.1 26.9 %copy-start.8 = (f32[4,2,256]{2,1,0:T(2,128)S(1)}, f32[4,2,256]{2,1,0:T(2,128)}, u32[]{:S(2)}) copy-start(f32[4,2,256]{2,1,0:T(2,128)} %get-tuple-element.55) | copy-start | bytes 24580
  284.1 27.8 %copy-start.3 = (f32[3,768]{1,0:T(4,128)S(1)}, f32[3,768]{1,0:T(4,128)}, u32[]{:S(2)}) copy-start(f32[3,768]{1,0:T(4,128)} %get-tuple-element.51) | copy-start | bytes 27652
  284.1 27.8 %copy-start.4 = (f32[3,768]{1,0:T(4,128)S(1)}, f32[3,768]{1,0:T(4,128)}, u32[]{:S(2)}) copy-start(f32[3,768]{1,0:T(4,128)} %get-tuple-element.52) | copy-start | bytes 27652
  307.5 112.6 %all-to-all-start.7 = ((bf16[2,1,196,768]{3,0,1,2:T(2,128)(2,1)}), bf16[2,1,196,768]{3,0,1,2:T(2,128)(2,1)S(1)}, u32[]{:S(2)}, u32[]{:S(2)}) async-start(bf16[2,1,196,768]{3,0,1,2:T(2,128)(2,1)} %copy.102), calls=%async_computation.7 | async-start | bytes 1204224 | tf_op jit(solution)/shard_map/all_to_all | solution.py:807
  312.8 2.3 copy-start
